TPU v7x, 32 devices: a whole 2x2x4 slice. The times are simulated.
32 devices in a mesh: section: 2 (over y), gy: 4 (over x, core), gx: 4 (over z).
Axes of the slice: x: 2, y: 2, z: 4, core: 2. Of those that a mesh axis runs over, the one named last changes fastest.
Arguments:
- streams: bfloat16 [2, 256, 256, 320], P('section', 'gy', 'gx'), may hold values from -24 to 24
- mask: int32 [256, 256], P('gy', 'gx'), may hold values 0 or 1
- timestep: int32 [1], replicated, may hold values from 0 to 999
- conv_weight: bfloat16 [2, 2, 3, 3, 320, 320], P('section'), may hold values from -0.109375 to 0.109375
- norm_gain: bfloat16 [2, 2, 320], P('section'), may hold values from 0.5 to 2
- time_weight: bfloat16 [2, 320, 320], P('section'), may hold values from -0.3125 to 0.3125
- cloud_vec: bfloat16 [2, 320], P('section'), may hold values from -4 to 4
- zero_weight: bfloat16 [320, 320], replicated, may hold values from -0.3125 to 0.3125
Outputs:
- conditioned: bfloat16 [256, 256, 320], P('gy', 'gx', 'section')
All inputs are finite; a program needn't handle non-finite values. No bound on the sum of `mask` on one device may be relied on, other than what follows from the above.
Results may differ from a plain program's by a relative error of at most 0.0065.
Values may be sent and summed in bfloat16 or wider, within the bound.
A program may use at most 128 MiB of HBM per device.

v0:
```python
import math

import jax
import jax.numpy as jnp
from jax import lax
from jax.sharding import PartitionSpec as P

GROUPS = 32


epsilon = 1e-05


def padded_2(x, sides, width):
    for axis, dim in sides:
        size, length = (lax.axis_size(axis), x.shape[dim])
        up = [(i, (i + 1) % size) for i in range(size - 1)]
        down = [(j, i) for i, j in up]
        last = lax.slice_in_dim(x, length - width, length, axis=dim)
        leading = lax.slice_in_dim(x, 0, width, axis=dim)
        before = lax.ppermute(last, axis, up)
        after = lax.ppermute(leading, axis, down)
        x = jnp.concatenate([before, x, after], axis=dim)
    return x


def conv_taps(padded, weight):
    out_height = padded.shape[0] - 2
    out_width = padded.shape[1] - 2
    channels = padded.shape[2]
    summed = jnp.zeros((out_height * out_width, weight.shape[3]), jnp.float32)
    for tap_row in range(3):
        for tap_col in range(3):
            window = padded[tap_row : tap_row + out_height, tap_col : tap_col + out_width].reshape(
                out_height * out_width, channels
            )
            summed = summed + jnp.dot(
                window, weight[tap_row, tap_col], preferred_element_type=jnp.float32
            )
    return summed.reshape(out_height, out_width, weight.shape[3])


def group_moments(interior):
    channels = interior.shape[-1]
    grouped = interior.reshape(-1, GROUPS, channels // GROUPS)
    count = grouped.shape[0] * grouped.shape[2] * lax.axis_size("gy") * lax.axis_size("gx")
    mean_value = lax.psum(jnp.sum(grouped, axis=(0, 2)), ("gy", "gx")) / count
    centered = grouped - mean_value[None, :, None]
    spread = lax.psum(jnp.sum(centered * centered, axis=(0, 2)), ("gy", "gx")) / count
    return (mean_value, lax.rsqrt(spread + epsilon))


def apply_norm(field, stats, gain):
    mean_value, inverse = stats
    full_shape = field.shape
    grouped = field.reshape(full_shape[:-1] + (GROUPS, full_shape[-1] // GROUPS))
    normed = (grouped - mean_value[:, None]) * inverse[:, None]
    return jax.nn.silu(normed.reshape(full_shape) * gain).astype(jnp.bfloat16)


def padded_once(field):
    return padded_2(field, (("gy", 0), ("gx", 1)), 1)


def per_device(
    streams, mask, timestep, conv_weight, norm_gain, time_weight, cloud_vec, zero_weight
):
    section_index = lax.axis_index("section")
    channels = streams.shape[-1]
    half_width = channels // 2
    freqs = jnp.exp(-math.log(10000.0) * jnp.arange(half_width, dtype=jnp.float32) / half_width)
    angles = timestep[0].astype(jnp.float32) * freqs
    sinus = jnp.concatenate([jnp.cos(angles), jnp.sin(angles)]).astype(jnp.bfloat16)
    embedded = jax.nn.silu(
        jnp.dot(sinus[None], time_weight[0], preferred_element_type=jnp.float32)
    )[0]
    flags = mask.astype(jnp.float32)[:, :, None]
    inputs = streams[0].astype(jnp.float32) + flags * cloud_vec[0].astype(jnp.float32)
    first_gain = norm_gain[0, 0].astype(jnp.float32)
    second_gain = norm_gain[0, 1].astype(jnp.float32)
    first = apply_norm(inputs, group_moments(inputs), first_gain)
    middle = conv_taps(padded_once(first), conv_weight[0, 0]) + embedded
    second = apply_norm(middle, group_moments(middle), second_gain)
    update = conv_taps(padded_once(second), conv_weight[0, 1])
    skip = (inputs + update).astype(jnp.bfloat16)
    residual = jnp.dot(
        skip.reshape(-1, channels), zero_weight, preferred_element_type=jnp.float32
    ).reshape(skip.shape)
    term = jnp.where(section_index == 0, residual, skip.astype(jnp.float32))
    total = lax.psum(term, "section")
    share = lax.dynamic_slice_in_dim(total, section_index * half_width, half_width, 2)
    return share.astype(jnp.bfloat16)


def solution(mesh):
    return jax.shard_map(
        per_device,
        mesh=mesh,
        in_specs=(
            P("section", "gy", "gx", None),
            P("gy", "gx"),
            P(),
            P("section", None, None, None, None, None),
            P("section", None, None),
            P("section", None, None),
            P("section", None),
            P(),
        ),
        out_specs=P("gy", "gx", "section"),
        check_vma=False,
    )
```

profile of v0, /device:TPU:0, one launch (start us, length us, event | category | flops | bytes accessed | tf_op | source)
XLA Modules:
  0.0 443.4 jit_solution(14184362716562202834)
XLA Ops:
  1.7 2.5 fusion.2
  4.4 35.1 %psum.35 = f32[32]{0:T(128)S(1)} all-reduce(f32[32]{0:T(128)S(1)} %reduce_sum.51), channel_id=1, replica_groups=mesh['section'=2,'gy'=4,'gx'=4] {'gy','gx'}, use_global_device_ids=true, to_apply=%region_2.3 | all-reduce | flops 32 | bytes 256 | tf_op jit(solution)/shard_map/psum | solution.py:47
  39.7 1.5 multiply_reduce_fusion
  41.4 29.7 %psum.36 = f32[32]{0:T(128)S(1)} all-reduce(f32[32]{0:T(128)S(1)} %reduce_sum.54), channel_id=1, replica_groups=mesh['section'=2,'gy'=4,'gx'=4] {'gy','gx'}, use_global_device_ids=true, to_apply=%region_5.6 | all-reduce | flops 32 | bytes 256 | tf_op jit(solution)/shard_map/psum | solution.py:49
  71.3 2.8 multiply_convert_fusion.2
  74.1 1.3 collective-permute-start
  76.7 3.7 multiply_convert_fusion.1
  80.4 4.1 slice_bitcast_fusion
  85.8 4.2 collective-permute-start.2
  91.2 2.3 pad_maximum_fusion.4
  93.6 3.9 fusion.11
  97.5 2.6 maximum_maximum_fusion
  100.1 8.2 %fusion.18 = (bf16[64,64,320]{2,1,0:T(8,128)(2,1)}, bf16[64,64,320]{2,1,0:T(8,128)(2,1)}, bf16[64,64,320]{2,1,0:T(8,128)(2,1)}, bf16[64,64,320]{2,1,0:T(8,128)(2...) fusion(bf16[66,65,320]{2,1,0:T(8,128)(2,1)S(1)} %get-tuple-element.25, ...), kind=kLoop, calls=%fused_computation.92 | loop fusion | bytes 31457280 | tf_op jit(solution)/shard_map/slice | solution.py:34
  108.3 2.7 fusion.10
  111.8 2.7 convolution_add_fusion.13
  114.6 1.6 convolution_add_fusion.12
  116.4 1.6 convolution_add_fusion.11
  118.1 3.6 convolution_add_fusion.10
  121.7 1.6 convolution_add_fusion.9
  123.6 1.6 convolution_add_fusion.8
  125.5 4.8 %add_reduce_fusion = (f32[320]{0:T(512)S(1)}, f32[4096,320]{0,1:T(8,128)}) fusion(f32[320]{0:T(512)S(1)} %divide_multiply_fusion, f32[4096,320]{0,1:T(8,128)S(1)} %fusion.10, f32[4096,320]{0,1:T(8,128)S(1)} %convolution_add_fusion.8, bf16[4096,320]{1,0:T(8,128)(2,1)S(1)} %bitcast.131, bf16[3,3,320,320]{3,2,1,0:T(8,128)(2,1)S(1)} %copy-done.13), kind=kOutput, calls=%fused_computation.28 | convolution fusion | flops 844103360 | bytes 19123456 | tf_op jit(solution)/shard_map/dot_general | solution.py:37
  130.5 32.3 %psum.37 = f32[32]{0:T(128)S(1)} all-reduce(f32[32]{0:T(128)S(1)} %reduce_sum.72), channel_id=1, replica_groups=mesh['section'=2,'gy'=4,'gx'=4] {'gy','gx'}, use_global_device_ids=true, to_apply=%region_8.9 | all-reduce | flops 32 | bytes 256 | tf_op jit(solution)/shard_map/psum | solution.py:47
  163.0 6.3 %copy.14 = f32[4096,320]{1,0:T(8,128)} copy(f32[4096,320]{0,1:T(8,128)} %get-tuple-element.38) | data formatting | bytes 10485760 | tf_op jit(solution)/shard_map/add | solution.py:37
  169.3 3.3 multiply_reduce_fusion.1
  172.9 29.7 %psum.38 = f32[32]{0:T(128)S(1)} all-reduce(f32[32]{0:T(128)S(1)} %reduce_sum.75), channel_id=1, replica_groups=mesh['section'=2,'gy'=4,'gx'=4] {'gy','gx'}, use_global_device_ids=true, to_apply=%region_11.12 | all-reduce | flops 32 | bytes 256 | tf_op jit(solution)/shard_map/psum | solution.py:49
  202.8 3.9 multiply_convert_fusion
  206.8 1.7 copy-done.2
  211.8 3.4 copy.13
  215.2 2.3 collective-permute-done.5
  217.5 1.3 pad_maximum_fusion.8
  218.8 4.2 collective-permute-start.6
  224.3 2.4 pad_maximum_fusion.2
  226.7 2.5 fusion.9
  229.5 2.6 maximum_maximum_fusion.1
  233.4 7.0 %fusion.17 = (bf16[64,64,320]{2,1,0:T(8,128)(2,1)}, bf16[64,64,320]{2,1,0:T(8,128)(2,1)S(1)}, bf16[64,64,320]{2,1,0:T(8,128)(2,1)S(1)}) fusion(bf16[66,65,320]{2,1,0:T(8,128)(2,1)S(1)} %get-tuple-element.22), kind=kLoop, calls=%fused_computation.91 | loop fusion | bytes 15728640 | tf_op jit(solution)/shard_map/slice | solution.py:34
  240.4 2.5 convolution_add_fusion.6
  242.9 2.7 convolution_add_fusion.5
  245.7 2.7 convolution_add_fusion.4
  248.4 6.0 %convolution_add_fusion = f32[4096,320]{0,1:T(8,128)} fusion(f32[4096,320]{0,1:T(8,128)S(1)} %convolution_add_fusion.4, f32[4096,320]{0,1:T(8,128)S(1)} %bitcast.122, f32[320]{0:T(512)S(1)} %get-tuple-element.5, f32[320]{0:T(512)S(1)} %copy-done.16, f32[320]{0:T(512)S(1)} %sub.54, f32[320]{0:T(512)S(1)} %divide_multiply_fusion, ...), kind=kOutput, calls=%fused_computation.8 | convolution fusion | flops 851968000 | bytes 15979520 | tf_op jit(solution)/shard_map/dot_general | solution.py:37
  254.4 2.7 fusion.8
  257.1 4.5 %convolution_add_fusion.3 = f32[4096,320]{0,1:T(8,128)S(1)} fusion(f32[4096,320]{0,1:T(8,128)} %convolution_add_fusion, bf16[4096,320]{1,0:T(8,128)(2,1)S(1)} %bitcast.134, bf16[3,3,320,320]{3,2,1,0:T(8,128)(2,1)} %get-tuple-element.7), kind=kOutput, calls=%fused_computation.11 | convolution fusion | flops 840171520 | bytes 13352960 | tf_op jit(solution)/shard_map/dot_general | solution.py:37
  261.6 2.6 convolution_add_fusion.2
  264.2 7.9 %add_convert_fusion.1 = (bf16[4096,320]{0,1:T(8,128)(2,1)}, f32[4096,320]{0,1:T(8,128)}) fusion(f32[4096,320]{0,1:T(8,128)S(1)} %bitcast.130, f32[320]{0:T(512)S(1)} %convert_reduce_fusion.2, f32[4096]{0:T(1024)S(1)} %mul.153, f32[4096,320]{0,1:T(8,128)S(1)} %fusion.8, f32[4096,320]{0,1:T(8,128)S(1)} %convolution_add_fusion.2, ...), kind=kOutput, calls=%fused_computation.24 | convolution fusion | flops 846725120 | bytes 27002112 | tf_op jit(solution)/shard_map/dot_general | solution.py:37
  272.1 6.3 %copy.16 = f32[4096,320]{1,0:T(8,128)} copy(f32[4096,320]{0,1:T(8,128)} %get-tuple-element.40) | data formatting | bytes 10485760 | tf_op jit(solution)/shard_map/add | solution.py:37
  278.5 4.6 %copy.15 = bf16[4096,320]{1,0:T(8,128)(2,1)} copy(bf16[4096,320]{0,1:T(8,128)(2,1)} %get-tuple-element.39) | data formatting | bytes 5242880 | tf_op jit(solution)/shard_map/convert_element_type | solution.py:85
  283.0 8.7 %convert_select_fusion = f32[64,64,320]{2,1,0:T(8,128)} fusion(f32[64,64,320]{2,1,0:T(8,128)} %bitcast.123, bf16[1,64,64,320]{3,2,1,0:T(8,128)(2,1)S(1)} %copy-done.1, f32[320]{0:T(512)S(1)} %convert_reduce_fusion.2, f32[64,64]{1,0:T(8,128)S(1)} %convert_element_type.75, pred[]{:T(512)S(6)} %eq.3, bf16[64,64,320]{2,1,0:T(8,128)(2,1)} %bitcast.142, ...), kind=kOutput, calls=%fused_computation.1 | convolution fusion | flops 848035840 | bytes 15951105 | tf_op jit(solution)/shard_map/dot_general | solution.py:86
  291.8 148.8 %all-reduce.1 = bf16[64,64,320]{2,1,0:T(8,128)(2,1)S(1)} all-reduce(f32[64,64,320]{2,1,0:T(8,128)} %convert_select_fusion), channel_id=1, replica_groups=mesh['section'=2,'gy'=4,'gx'=4] {'section'}, use_global_device_ids=true, to_apply=%region_12.13 | all-reduce | flops 1310720 | bytes 7864320 | tf_op jit(solution)/shard_map/psum | solution.py:90
  440.5 2.4 dynamic-slice_convert_fusion
  (90 shorter events, 14.3 us)
Async XLA Ops:
  0.0 283.0 %copy-start = (bf16[320,320]{1,0:T(8,128)(2,1)S(1)}, bf16[320,320]{1,0:T(8,128)(2,1)}, u32[]{:S(2)}) copy-start(bf16[320,320]{1,0:T(8,128)(2,1)} %param.15) | copy-start | bytes 614404
  0.0 39.7 %copy-start.1 = (bf16[1,64,64,320]{3,2,1,0:T(8,128)(2,1)S(1)}, bf16[1,64,64,320]{3,2,1,0:T(8,128)(2,1)}, u32[]{:S(2)}) copy-start(bf16[1,64,64,320]{3,2,1,0:T(8,128)(2,1)} %param.8) | copy-start | bytes 7864324
  0.0 71.3 %copy-start.17 = (bf16[1,2,320]{2,1,0:T(2,128)(2,1)S(1)}, bf16[1,2,320]{2,1,0:T(2,128)(2,1)}, u32[]{:S(2)}) copy-start(bf16[1,2,320]{2,1,0:T(2,128)(2,1)} %param.12) | copy-start | bytes 3844
  74.1 11.4 %collective-permute-start = (bf16[1,64,320]{2,1,0:T(8,128)(2,1)S(1)}, bf16[1,64,320]{2,1,0:T(8,128)(2,1)S(1)}, u32[]{:S(2)}, u32[]{:S(2)}) collective-permute-start(bf16[1,64,320]{2,1,0:T(8,128)(2,1)S(1)} %get-tuple-element.35), channel_id=1, source_target_pairs={{0,4},{4,8},{8,12},{1,5},{5,9},{9,13},{2,6},{6,10},{10,14},{3,7},{... | collective-permute-start | bytes 122888 | tf_op jit(solution)/shard_map/ppermute | solution.py:21
  75.4 10.1 %collective-permute-start.1 = (bf16[1,64,320]{2,1,0:T(8,128)(2,1)S(1)}, bf16[1,64,320]{2,1,0:T(8,128)(2,1)S(1)}, u32[]{:S(2)}, u32[]{:S(2)}) collective-permute-start(bf16[1,64,320]{2,1,0:T(8,128)(2,1)S(1)} %get-tuple-element.36), channel_id=1, source_target_pairs={{4,0},{8,4},{12,8},{5,1},{9,5},{13,9},{6,2},{10,6},{14,10},{7,3},{... | collective-permute-start | bytes 122888 | tf_op jit(solution)/shard_map/ppermute | solution.py:22
  80.4 4.9 %copy-start.14 = (bf16[1,320,320]{2,1,0:T(8,128)(2,1)S(1)}, bf16[1,320,320]{2,1,0:T(8,128)(2,1)}, u32[]{:S(2)}) copy-start(bf16[1,320,320]{2,1,0:T(8,128)(2,1)} %param.13) | copy-start | bytes 614404
  84.6 9.0 %copy-start.12 = (bf16[3,3,320,320]{3,2,1,0:T(8,128)(2,1)}, bf16[3,3,320,320]{3,2,1,0:T(8,128)(2,1)S(1)}, u32[]{:S(2)}) copy-start(bf16[3,3,320,320]{3,2,1,0:T(8,128)(2,1)S(1)} %get-tuple-element.8) | copy-start | bytes 5529604
  85.8 11.7 %collective-permute-start.2 = (bf16[66,1,320]{2,1,0:T(2,128)(2,1)S(1)}, bf16[66,1,320]{2,1,0:T(2,128)(2,1)S(1)}, u32[]{:S(2)}, u32[]{:S(2)}) collective-permute-start(bf16[66,1,320]{2,1,0:T(2,128)(2,1)S(1)} %get-tuple-element.27), channel_id=1, source_target_pairs={{0,1},{1,2},{2,3},{4,5},{5,6},{6,7},{8,9},{9,10},{10,11},{12,13},{... | collective-permute-start | bytes 126728 | tf_op jit(solution)/shard_map/ppermute | solution.py:21
  89.9 7.5 %collective-permute-start.3 = (bf16[66,1,320]{2,1,0:T(2,128)(2,1)S(1)}, bf16[66,1,320]{2,1,0:T(2,128)(2,1)S(1)}, u32[]{:S(2)}, u32[]{:S(2)}) collective-permute-start(bf16[66,1,320]{2,1,0:T(2,128)(2,1)S(1)} %get-tuple-element.28), channel_id=1, source_target_pairs={{1,0},{2,1},{3,2},{5,4},{6,5},{7,6},{9,8},{10,9},{11,10},{13,12},{... | collective-permute-start | bytes 126728 | tf_op jit(solution)/shard_map/ppermute | solution.py:22
  108.2 2.7 copy-start.4
  108.3 3.6 copy-start.11
  111.8 2.7 copy-start.10
  111.8 2.7 copy-start.13
  114.5 1.9 copy-start.9
  118.1 3.6 copy-start.8
  121.7 1.9 copy-start.6
  123.6 1.9 copy-start.5
  202.8 7.6 %copy-start.15 = (f32[320]{0:T(512)}, f32[320]{0:T(512)S(1)}, u32[]{:S(2)}) copy-start(f32[320]{0:T(512)S(1)} %mul.183) | copy-start | bytes 3844
  206.7 1.7 copy-start.2
  209.1 6.1 %collective-permute-start.4 = (bf16[1,64,320]{2,1,0:T(8,128)(2,1)}, bf16[1,64,320]{2,1,0:T(8,128)(2,1)S(1)}, u32[]{:S(2)}, u32[]{:S(2)}) collective-permute-start(bf16[1,64,320]{2,1,0:T(8,128)(2,1)} %get-tuple-element.31), channel_id=1, source_target_pairs={{0,4},{4,8},{8,12},{1,5},{5,9},{9,13},{2,6},{6,10},{10,14},{3,7},{... | collective-permute-start | bytes 122888 | tf_op jit(solution)/shard_map/ppermute | solution.py:21
  210.4 7.1 %collective-permute-start.5 = (bf16[1,64,320]{2,1,0:T(8,128)(2,1)}, bf16[1,64,320]{2,1,0:T(8,128)(2,1)S(1)}, u32[]{:S(2)}, u32[]{:S(2)}) collective-permute-start(bf16[1,64,320]{2,1,0:T(8,128)(2,1)} %get-tuple-element.32), channel_id=1, source_target_pairs={{4,0},{8,4},{12,8},{5,1},{9,5},{13,9},{6,2},{10,6},{14,10},{7,3},{... | collective-permute-start | bytes 122888 | tf_op jit(solution)/shard_map/ppermute | solution.py:22
  215.2 9.1 %copy-start.3 = (bf16[64,64,320]{2,1,0:T(8,128)(2,1)S(1)}, bf16[64,64,320]{2,1,0:T(8,128)(2,1)}, u32[]{:S(2)}) copy-start(bf16[64,64,320]{2,1,0:T(8,128)(2,1)} %copy-done.2) | copy-start | bytes 7864324
  218.8 10.4 %collective-permute-start.6 = (bf16[66,1,320]{2,1,0:T(2,128)(2,1)S(1)}, bf16[66,1,320]{2,1,0:T(2,128)(2,1)S(1)}, u32[]{:S(2)}, u32[]{:S(2)}) collective-permute-start(bf16[66,1,320]{2,1,0:T(2,128)(2,1)S(1)} %get-tuple-element.23), channel_id=1, source_target_pairs={{0,1},{1,2},{2,3},{4,5},{5,6},{6,7},{8,9},{9,10},{10,11},{12,13},{... | collective-permute-start | bytes 126728 | tf_op jit(solution)/shard_map/ppermute | solution.py:21
  223.0 6.5 %collective-permute-start.7 = (bf16[66,1,320]{2,1,0:T(2,128)(2,1)S(1)}, bf16[66,1,320]{2,1,0:T(2,128)(2,1)S(1)}, u32[]{:S(2)}, u32[]{:S(2)}) collective-permute-start(bf16[66,1,320]{2,1,0:T(2,128)(2,1)S(1)} %get-tuple-element.24), channel_id=1, source_target_pairs={{1,0},{2,1},{3,2},{5,4},{6,5},{7,6},{9,8},{10,9},{11,10},{13,12},{... | collective-permute-start | bytes 126728 | tf_op jit(solution)/shard_map/ppermute | solution.py:22
  242.9 5.5 %slice-start = ((s8[5242880]{0:T(1024)(128)(4,1)}), s8[4194304]{0:T(1024)(128)(4,1)S(1)}, s32[]{:S(2)}) async-start(s8[5242880]{0:T(1024)(128)(4,1)} %bitcast.121), calls=%async_computation | async-start | bytes 8388608
  245.6 2.7 slice-start.1
  245.6 2.7 copy-start.16
  254.4 2.7 copy-start.7
  257.1 7.1 %slice-start.2 = ((s8[5242880]{0:T(1024)(128)(4,1)}), s8[4194304]{0:T(1024)(128)(4,1)S(1)}, s32[]{:S(2)}) async-start(s8[5242880]{0:T(1024)(128)(4,1)} %bitcast.129), calls=%async_computation.2 | async-start | bytes 8388608
  261.6 2.6 slice-start.3
where the time goes:
time: 452 us; the launch traced here: 443 us
  blocking collectives  276 us (61%)
  matrix products  67.1 us (15%)
  local copies, waits for them, and re-layouts  48.9 us (11%)
  other arithmetic  31.4 us (7%)
  starting transfers between devices  16 us (4%)
    psum x1, blocking collectives, per_device(): total = lax.psum(term, 'section')  149 us
    psum x2, blocking collectives, group_moments(): mean_value = lax.psum(jnp.sum(grouped, axis=(0, 2)), ('gy', 'gx')) / count  67.4 us
    psum x2, blocking collectives, group_moments(): lax.psum(jnp.sum(centered * centered, axis=(0, 2)), ('gy', 'gx')) / count  59.4 us
    dot_general x18, matrix products, conv_taps(): jnp.dot(window, weight[tap_row, tap_col], preferred_element_type=jnp.floa...  58.2 us
    slice x3, local copies, waits for them, and re-layouts, conv_taps(): padded[tap_row:tap_row + out_height, tap_col:tap_col + out_width]  16.4 us
    add x2, local copies, waits for them, and re-layouts, conv_taps(): summed + jnp.dot(window, weight[tap_row, tap_col], preferred_element_type...  12.7 us
    ppermute x4, starting transfers between devices, padded_2(): before = lax.ppermute(last, axis, up)  10.9 us
    convert_element_type x3, other arithmetic, apply_norm(): return jax.nn.silu(normed.reshape(full_shape) * gain).astype(jnp.bfloat16)  10.4 us
  transfers between devices with their start and end apart: 8, of which 2 were waited for; matrix products, arithmetic and copies ran while one was open for 5% of the time, Pallas kernels for 0%

commit v1 on v0

v1 whole, which is shorter than its diff:
```python
import functools
import math

import jax
import jax.numpy as jnp
from jax import lax
from jax.experimental import pallas as pl
from jax.experimental.pallas import tpu as pltpu
from jax.sharding import PartitionSpec as P

GROUPS = 32
EPS = 1e-05
ROWS = 8
MESH = pl.DeviceIdType.MESH
VMEM = pltpu.VMEM
SPLITS = 2


def vspec(count):
    return [pl.BlockSpec(memory_space=VMEM)] * count


def f32(*shape):
    return jax.ShapeDtypeStruct(shape, jnp.float32)


def bf16(*shape):
    return jax.ShapeDtypeStruct(shape, jnp.bfloat16)


def load_inputs(x_ref, mask_ref, cloud_ref, start, count):
    channels = x_ref.shape[1]
    x = x_ref[pl.ds(start, count), :].astype(jnp.float32)
    m = mask_ref[pl.ds(start, count), :].astype(jnp.float32)
    m = jnp.concatenate([m] * pl.cdiv(channels, 128), axis=1)[:, :channels]
    return x + m * cloud_ref[...]


def merge_stats(stat_ref, t, index):
    cells = t.shape[0]
    mean = jnp.sum(t, axis=0, keepdims=True) / cells
    diff = t - mean
    square = jnp.sum(diff * diff, axis=0, keepdims=True)
    k = jnp.asarray(index, jnp.float32)
    delta = mean - stat_ref[0:1, :]
    stat_ref[0:1, :] = stat_ref[0:1, :] + delta / (k + 1.0)
    stat_ref[1:2, :] = stat_ref[1:2, :] + square + delta * delta * (cells * k / (k + 1.0))


def store_columns(t, width, left_ref, right_ref, index):
    t3 = t.reshape(ROWS, width, t.shape[1])
    at = pl.ds(pl.multiple_of(index * ROWS, ROWS), ROWS)
    left_ref[at, :] = t3[:, 0, :]
    right_ref[at, :] = t3[:, width - 1, :]


def stats_kernel(height, width, x_ref, mask_ref, cloud_ref, stat_ref, top_ref, bot_ref, left_ref, right_ref):
    stat_ref[...] = jnp.zeros_like(stat_ref)
    cells = ROWS * width

    def body(i, carry):
        t = load_inputs(x_ref, mask_ref, cloud_ref, pl.multiple_of(i * cells, cells), cells)
        merge_stats(stat_ref, t, i)
        store_columns(t, width, left_ref, right_ref, i)
        return carry

    lax.fori_loop(0, height // ROWS, body, 0)
    top_ref[...] = load_inputs(x_ref, mask_ref, cloud_ref, 0, width)
    bot_ref[...] = load_inputs(x_ref, mask_ref, cloud_ref, (height - 1) * width, width)


def exchange_kernel(ny, nx, stat, top, bot, left, right, gathered, up, down, lft, rgt, corner, send, recv):
    me_y, me_x = lax.axis_index("gy"), lax.axis_index("gx")
    n = ny * nx

    def peer(d):
        y = lax.rem(me_y + d // nx, ny)
        x = lax.rem(me_x + d % nx, nx)
        return {"gy": y, "gx": x}

    def near(dy, dx):
        return {"gy": lax.rem(me_y + dy + ny, ny), "gx": lax.rem(me_x + dx + nx, nx)}

    barrier = pltpu.get_barrier_semaphore()
    for d in range(1, n):
        pl.semaphore_signal(barrier, inc=1, device_id=peer(d), device_id_type=MESH)
    pl.semaphore_wait(barrier, n - 1)
    width = top.shape[0]
    first, last = pl.ds(0, 8), pl.ds(width - 8, 8)
    jobs = [(stat, gathered.at[d], peer(d)) for d in range(1, n)]
    jobs += [
        (bot, up, near(1, 0)),
        (top, down, near(-1, 0)),
        (right, lft, near(0, 1)),
        (left, rgt, near(0, -1)),
        (bot.at[last], corner.at[0], near(1, 1)),
        (bot.at[first], corner.at[1], near(1, -1)),
        (top.at[last], corner.at[2], near(-1, 1)),
        (top.at[first], corner.at[3], near(-1, -1)),
    ]
    copies = []
    for k, (src, dst, target) in enumerate(jobs):
        copy = pltpu.make_async_remote_copy(
            src_ref=src, dst_ref=dst, send_sem=send.at[k], recv_sem=recv.at[k],
            device_id=target, device_id_type=MESH,
        )
        copy.start()
        copies.append(copy)
    gathered[0] = stat[...]
    for copy in copies:
        copy.wait()


def exchange(ny, nx, stat, top, bot, left, right):
    width, channels = top.shape
    height = left.shape[0]
    count = ny * nx - 1 + 8
    return pl.pallas_call(
        functools.partial(exchange_kernel, ny, nx),
        out_shape=(
            f32(ny * nx, 8, channels), f32(width, channels), f32(width, channels),
            f32(height, channels), f32(height, channels), f32(4, 8, channels),
        ),
        in_specs=vspec(5),
        out_specs=tuple(vspec(6)),
        scratch_shapes=[pltpu.SemaphoreType.DMA((count,)), pltpu.SemaphoreType.DMA((count,))],
        compiler_params=pltpu.CompilerParams(collective_id=0, has_side_effects=True),
        name="exchange",
    )(stat, top, bot, left, right)


def group_factors(g_ref, group_ref, gain_ref, cells):
    n = g_ref.shape[0]
    channels = g_ref.shape[2]
    per = channels // GROUPS
    means = g_ref[:, 0, :]
    squares = g_ref[:, 1, :]

    def spread(v):
        v8 = jnp.broadcast_to(v, (8, channels))
        return jnp.dot(v8, group_ref[...], precision=lax.Precision.HIGHEST,
                       preferred_element_type=jnp.float32)[0:1, :]

    mean = spread(jnp.sum(means, axis=0, keepdims=True) / n) / per
    off = means - mean
    total = jnp.sum(squares, axis=0, keepdims=True) + cells * jnp.sum(off * off, axis=0, keepdims=True)
    var = spread(total) / (float(cells) * n * per)
    return mean, lax.rsqrt(var + EPS) * gain_ref[...]


def fill_columns(q_ref, start, act, lcol, rcol, rows, width):
    channels = act.shape[1]
    v = act.reshape(rows, width, channels)
    col = lax.broadcasted_iota(jnp.int32, v.shape, 1)
    vl = jnp.where(col == 0, lcol.reshape(rows, 1, channels), pltpu.roll(v, 1, 1))
    vr = jnp.where(col == width - 1, rcol.reshape(rows, 1, channels), pltpu.roll(v, width - 1, 1))
    for k, part in enumerate((vl, v, vr)):
        q_ref[pl.ds(start, rows * width), k * channels:(k + 1) * channels] = part.reshape(
            rows * width, channels
        ).astype(jnp.bfloat16)


def fill(q_ref, flags, load, halos, mean, scale, height, width, row0, rows):
    up, down, lft, rgt, corner = halos

    def act(t, valid=None):
        z = (t - mean) * scale
        z = z / (1.0 + jnp.exp(-z))
        return z if valid is None else jnp.where(valid, z, 0.0)

    has_up, has_down, has_left, has_right = [flags[k] > 0 for k in range(4)]

    def body(i, carry):
        at = pl.ds(pl.multiple_of(row0 + i * ROWS, ROWS), ROWS)
        cells = ROWS * width
        t = load(pl.multiple_of(row0 * width + i * cells, width), cells)
        start = pl.multiple_of((1 + i * ROWS) * width, width)
        fill_columns(q_ref, start, act(t), act(lft[at, :], has_left), act(rgt[at, :], has_right), ROWS, width)
        return carry

    lax.fori_loop(0, rows // ROWS, body, 0)

    def single(slot, row):
        if row < 0:
            t, valid, lcol, rcol = up[...], has_up, corner[0, 7:8, :], corner[1, 0:1, :]
        elif row >= height:
            t, valid, lcol, rcol = down[...], has_down, corner[2, 7:8, :], corner[3, 0:1, :]
        else:
            t, valid, lcol, rcol = load(row * width, width), True, lft[row:row + 1, :], rgt[row:row + 1, :]
        fill_columns(
            q_ref, slot * width, act(t) if valid is True else act(t, valid),
            act(lcol, has_left & valid), act(rcol, has_right & valid), 1, width,
        )

    single(0, row0 - 1)
    single(rows + 1, row0 + rows)


def conv_chunk(q_ref, w_ref, i, width):
    cells = ROWS * width
    total = None
    for dy in range(3):
        part = jnp.dot(
            q_ref[pl.ds(pl.multiple_of((i * ROWS + dy) * width, width), cells), :],
            w_ref[dy], preferred_element_type=jnp.float32,
        )
        total = part if total is None else total + part
    return total


def first_kernel(height, width, flags, x_ref, mask_ref, cloud_ref, g_ref, up, down, lft, rgt, corner,
                 gain_ref, group_ref, embed_ref, w_ref,
                 mid_ref, stat_ref, top_ref, bot_ref, left_ref, right_ref, q_ref):
    mean, scale = group_factors(g_ref, group_ref, gain_ref, height * width)
    load = functools.partial(load_inputs, x_ref, mask_ref, cloud_ref)
    fill(q_ref, flags, load, (up, down, lft, rgt, corner), mean, scale, height, width, 0, height)
    stat_ref[...] = jnp.zeros_like(stat_ref)
    cells = ROWS * width

    def body(i, carry):
        t = conv_chunk(q_ref, w_ref, i, width) + embed_ref[...]
        mid_ref[pl.ds(pl.multiple_of(i * cells, cells), cells), :] = t
        merge_stats(stat_ref, t, i)
        store_columns(t, width, left_ref, right_ref, i)
        return carry

    lax.fori_loop(0, height // ROWS, body, 0)
    top_ref[...] = mid_ref[0:width, :]
    bot_ref[...] = mid_ref[(height - 1) * width:, :]


def second_kernel(height, width, row0, rows, flags, x_ref, mask_ref, cloud_ref, mid_ref, g_ref, up, down, lft,
                  rgt, corner, gain_ref, group_ref, w_ref, mix_ref,
                  keep_ref, send_ref, rest_ref, q_ref):
    mean, scale = group_factors(g_ref, group_ref, gain_ref, height * width)
    fill(q_ref, flags, lambda s, n: mid_ref[pl.ds(s, n), :], (up, down, lft, rgt, corner),
         mean, scale, height, width, row0, rows)
    cells = ROWS * width
    quarter = cells // 4
    half = keep_ref.shape[1]

    def body(i, carry):
        at = pl.ds(pl.multiple_of(i * cells, cells), cells)
        t = load_inputs(x_ref, mask_ref, cloud_ref, pl.multiple_of(row0 * width + i * cells, width), cells)
        skip = (t + conv_chunk(q_ref, w_ref, i, width)).astype(jnp.bfloat16)
        y = jnp.dot(skip, mix_ref[...], preferred_element_type=jnp.float32)
        keep_ref[at, :] = y[:, :half]
        send_ref[at, :] = y[:, 256:384].astype(jnp.bfloat16)
        lane = lax.broadcasted_iota(jnp.int32, (quarter, 128), 1)
        rest = y[0:quarter, 384:512]
        for k in range(1, 4):
            rest = jnp.where(lane >= 32 * k, y[k * quarter:(k + 1) * quarter, 384:512], rest)
        rest_ref[pl.ds(pl.multiple_of(i * quarter, quarter), quarter), :] = rest.astype(jnp.bfloat16)
        return carry

    lax.fori_loop(0, rows // ROWS, body, 0)


def final_kernel(parts, quarter, *refs):
    out_ref = refs[-1]
    size = out_ref.shape[0] // parts
    for p in range(parts):
        keep_ref, got_ref, rest_ref = refs[3 * p:3 * p + 3]

        def body(i, carry):
            rest = rest_ref[pl.ds(pl.multiple_of(i * quarter, quarter), quarter), :].astype(jnp.float32)
            for k in range(4):
                start = pl.multiple_of(i * 4 * quarter + k * quarter, quarter)
                at = pl.ds(start, quarter)
                got = jnp.concatenate(
                    [got_ref[at, :].astype(jnp.float32), rest[:, 32 * k:32 * k + 32]], axis=1
                )
                out_ref[pl.ds(p * size + start, quarter), :] = (keep_ref[at, :] + got).astype(jnp.bfloat16)
            return carry

        lax.fori_loop(0, size // (4 * quarter), body, 0)


def per_device(streams, mask, timestep, conv_weight, norm_gain, time_weight, cloud_vec, zero_weight):
    section = lax.axis_index("section")
    iy, ix = lax.axis_index("gy"), lax.axis_index("gx")
    ny, nx = lax.axis_size("gy"), lax.axis_size("gx")
    height, width, channels = streams.shape[1:]
    cells = height * width
    half = channels // 2
    freqs = jnp.exp(-math.log(10000.0) * jnp.arange(half, dtype=jnp.float32) / half)
    angles = timestep[0].astype(jnp.float32) * freqs
    sinus = jnp.concatenate([jnp.cos(angles), jnp.sin(angles)]).astype(jnp.bfloat16)
    embed = jax.nn.silu(jnp.dot(sinus[None], time_weight[0], preferred_element_type=jnp.float32))
    x = streams.reshape(cells, channels)
    maskb = jnp.broadcast_to(mask.astype(jnp.bfloat16).reshape(cells, 1), (cells, 128))
    cloud = cloud_vec.astype(jnp.float32)
    gains = norm_gain[0].astype(jnp.float32)
    weights = conv_weight.reshape(2, 3, 3 * channels, channels)
    ids = jnp.arange(channels) // (channels // GROUPS)
    group = (ids[:, None] == ids[None, :]).astype(jnp.float32)
    flags = jnp.stack([iy > 0, iy < ny - 1, ix > 0, ix < nx - 1]).astype(jnp.int32)
    eye = (jnp.arange(channels)[:, None] == (jnp.arange(channels)[None, :] + half) % channels)
    mix = jnp.where(section == 0, zero_weight, eye.astype(jnp.bfloat16))
    tail = mix[:, half + 128:]
    mix = jnp.concatenate(
        [mix[:, :half], jnp.zeros((channels, 256 - half), jnp.bfloat16), mix[:, half:half + 128]] + [tail] * 4, axis=1
    )
    edges = (f32(8, channels), f32(width, channels), f32(width, channels), f32(height, channels), f32(height, channels))
    params = pltpu.CompilerParams(vmem_limit_bytes=50 << 20)

    first_edges = pl.pallas_call(
        functools.partial(stats_kernel, height, width),
        out_shape=edges, in_specs=vspec(3), out_specs=tuple(vspec(5)),
        compiler_params=params, name="stats",
    )(x, maskb, cloud)
    got = exchange(ny, nx, *first_edges)
    smem = [pl.BlockSpec(memory_space=pltpu.SMEM)]
    mid, *second_edges = pl.pallas_call(
        functools.partial(first_kernel, height, width),
        out_shape=(f32(cells, channels),) + edges,
        in_specs=smem + vspec(13), out_specs=tuple(vspec(6)),
        scratch_shapes=[VMEM(((height + 2) * width, 3 * channels), jnp.bfloat16)],
        compiler_params=params, name="first",
    )(flags, x, maskb, cloud, *got, gains[0:1], group, embed, weights[0])
    got = exchange(ny, nx, *second_edges)
    rows = height // SPLITS
    part = rows * width
    swap = [(0, 1), (1, 0)]
    finals = []
    for p in range(SPLITS):
        keep, send, rest = pl.pallas_call(
            functools.partial(second_kernel, height, width, p * rows, rows),
            out_shape=(f32(part, half), bf16(part, 128), bf16(part // 4, 128)),
            in_specs=smem + vspec(14), out_specs=tuple(vspec(3)),
            scratch_shapes=[VMEM(((rows + 2) * width, 3 * channels), jnp.bfloat16)],
            compiler_params=params, name="second",
            cost_estimate=pl.CostEstimate(
                flops=2 * 12 * part * 256 * 512, bytes_accessed=8 << 20, transcendentals=part * channels
            ),
        )(flags, x, maskb, cloud, mid, *got, gains[1:2], group, weights[1], mix)
        finals += [keep, lax.ppermute(send, "section", swap), lax.ppermute(rest, "section", swap)]
    out = pl.pallas_call(
        functools.partial(final_kernel, SPLITS, ROWS * width // 4),
        out_shape=bf16(cells, half), in_specs=vspec(3 * SPLITS),
        out_specs=pl.BlockSpec(memory_space=VMEM), compiler_params=params, name="final",
    )(*finals)
    return out.reshape(height, width, half)


def solution(mesh):
    return jax.shard_map(
        per_device,
        mesh=mesh,
        in_specs=(
            P("section", "gy", "gx", None),
            P("gy", "gx"),
            P(),
            P("section", None, None, None, None, None),
            P("section", None, None),
            P("section", None, None),
            P("section", None),
            P(),
        ),
        out_specs=P("gy", "gx", "section"),
        check_vma=False,
    )
```

time: 452 us -> 152 us (0.34); the launches traced: 443 us -> 151 us
  blocking collectives: 276 us -> 0 us
  Pallas kernels: 0 us -> 102 us
  matrix products: 67.1 us -> 0.17 us
  other arithmetic: 31.4 us -> 2.9 us
  local copies, waits for them, and re-layouts: 48.9 us -> 24.4 us
  waiting for transfers between devices: 2.64 us -> 16.3 us
  starting transfers between devices: 16 us -> 4.07 us
    psum x5 -> x0, blocking collectives: 276 us -> none  [the longest x1 149 us: per_device(): total = lax.psum(term, 'section')]
    pallas_call x0 -> x7, Pallas kernels: none -> 102 us  [the longest x2 33.8 us: exchange(): pl.pallas_call(functools.partial(exchange_kernel, ny, nx), out_shape=(f32...]
    dot_general x19 -> x0, matrix products: 67 us -> none  [the longest x18 58.2 us: conv_taps(): jnp.dot(window, weight[tap_row, tap_col], preferred_element_type=jnp.floa...]
    unnamed x44 -> x60, local copies, waits for them, and re-layouts: 3.52 us -> 18.4 us
    ppermute x8 -> x4, waiting for transfers between devices: 2.64 us -> 16.3 us  [the longest x2 16.3 us: per_device(): lax.ppermute(rest, 'section', swap)]
    add x2 -> x0, local copies, waits for them, and re-layouts: 12.7 us -> none  [conv_taps(): summed + jnp.dot(window, weight[tap_row, tap_col], preferred_element_type...]
    ppermute x8 -> x4, starting transfers between devices: 16 us -> 4.07 us  [the longest x2 2.04 us: per_device(): lax.ppermute(send, 'section', swap)]
    slice x5 -> x4, local copies, waits for them, and re-layouts: 17 us -> 5.09 us  [the longest x1 4.88 us: per_device(): weights[1]]
  transfers between devices with their start and end apart: 8 -> 4, of which waited for: 2 -> 2; matrix products, arithmetic and copies ran while one was open for 5% -> 0% of each run, Pallas kernels for 0% -> 11%
where the time goes in v1:
time: 152 us; the launch traced here: 151 us
  Pallas kernels  102 us (67%)
  local copies, waits for them, and re-layouts  24.4 us (16%)
  waiting for transfers between devices  16.3 us (11%)
  starting transfers between devices  4.07 us (3%)
  other arithmetic  2.9 us (2%)
    pallas_call x2, Pallas kernels, exchange(): pl.pallas_call(functools.partial(exchange_kernel, ny, nx), out_shape=(f32...  33.8 us
    pallas_call x2, Pallas kernels, per_device(): pl.pallas_call(functools.partial(second_kernel, height, width, p * rows,...  33.8 us
    pallas_call x1, Pallas kernels, per_device(): pl.pallas_call(functools.partial(first_kernel, height, width), out_shape=...  26.3 us
    unnamed x60, local copies, waits for them, and re-layouts  18.4 us
    ppermute x2, waiting for transfers between devices, per_device(): lax.ppermute(rest, 'section', swap)  16.3 us
    slice x1, local copies, waits for them, and re-layouts, per_device(): weights[1]  4.88 us
    pallas_call x1, Pallas kernels, per_device(): pl.pallas_call(functools.partial(stats_kernel, height, width), out_shape=...  4.66 us
    pallas_call x1, Pallas kernels, per_device(): pl.pallas_call(functools.partial(final_kernel, SPLITS, ROWS * width // 4)...  3.71 us
  transfers between devices with their start and end apart: 4, of which 2 were waited for; matrix products, arithmetic and copies ran while one was open for 0% of the time, Pallas kernels for 11%

profile of v1, /device:TPU:0, one launch (start us, length us, event | category | flops | bytes accessed | tf_op | source)
XLA Modules:
  0.0 151.0 jit_solution(4591264444388714837)
XLA Ops:
  0.0 1.1 fusion.1
  1.1 0.1 fusion.10
  1.3 0.1 slice.45
  1.4 0.8 convert_element_type.32
  2.1 0.1 broadcast_in_dim.6
  2.2 0.7 convert_element_type.33.cloud_ref
  2.9 0.1 compare_convert_fusion.group_ref
  3.7 0.1 pad_maximum_fusion
  3.8 0.2 convolution_reduce_fusion
  4.0 4.9 %fusion.9 = (bf16[1,1,3,3,320,320]{5,4,3,2,1,0:T(8,128)(2,1)}, bf16[1,1,3,3,320,320]{5,4,3,2,1,0:T(8,128)(2,1)}) fusion(bf16[1,2,3,3,320,320]{5,4,3,2,1,0:T(8,128)(2,1)} %param.11), kind=kLoop, calls=%fused_computation.26 | loop fusion | bytes 7372800 | tf_op jit(solution)/shard_map/slice | solution.py:336
  8.9 0.6 broadcast_in_dim.7.mask_ref
  9.5 4.7 %stats.1 = (f32[8,320]{1,0:T(8,128)S(1)}, f32[64,320]{1,0:T(8,128)S(1)}, f32[64,320]{1,0:T(8,128)S(1)}, f32[64,320]{1,0:T(8,128)S(1)}, f32[64,320]{1,0:T(8,128)S(1)}) custom-call(bf16[4096,320]{1,0:T(8,128)(2,1)} %bitcast.17, bf16[4096,128]{1,0:T(8,128)(2,1)S(1)} %broadcast_in_dim.7.mask_ref, f32[1,320]{1,0:T(1,128)S(1)} %convert_element_type.33.cloud_ref), custom_call_target="tpu_custom_call" | custom-call | tf_op jit(solution)/shard_map/stats/pallas_call | solution.py:307
  14.2 0.6 copy-done.7
  14.8 0.6 copy-done.8
  15.5 0.6 copy-done.9
  16.1 0.6 copy-done.10
  16.8 0.5 copy-done.16
  17.3 0.2 concatenate.9.mix_ref
  17.6 18.0 %exchange.2 = (f32[16,8,320]{2,1,0:T(8,128)}, f32[64,320]{1,0:T(8,128)}, f32[64,320]{1,0:T(8,128)}, f32[64,320]{1,0:T(8,128)}, f32[64,320]{1,0:T(8,128)}, /*index=5*/f32[4,8,320]{2,1,0:T(8,128)}) custom-call(f32[8,320]{1,0:T(8,128)} %copy-done.16, f32[64,320]{1,0:T(8,128)} %copy-done.7, f32[64,320]{1,0:T(8,128)} %copy-done.8, f32[64,320]{1,0:T(8,128)} %copy-done.9, ...), custom_call_target="tpu_custom_call" | custom-call | tf_op jit(solution)/shard_map/exchange/pallas_call | solution.py:118
  35.6 0.9 copy-done.2
  36.5 0.9 copy-done.3
  37.4 0.9 copy-done.4
  38.3 0.9 copy-done.5
  39.2 0.9 copy-done.6
  40.1 0.8 copy-done.15
  40.9 26.3 %first.1 = (f32[4096,320]{1,0:T(8,128)}, f32[8,320]{1,0:T(8,128)S(1)}, f32[64,320]{1,0:T(8,128)S(1)}, f32[64,320]{1,0:T(8,128)S(1)}, f32[64,320]{1,0:T(8,128)S(1)}, /*index=5*/f32[64,320]{1,0:T(8,128)S(1)}) custom-call(s32[4]{0:T(128)S(1)} %add_convert_fusion.flags, bf16[4096,320]{1,0:T(8,128)(2,1)} %bitcast.18, ...), custom_call_target="tpu_custom_call" | custom-call | tf_op jit(solution)/shard_map/first/pallas_call | solution.py:314
  67.2 0.6 copy-done.11
  67.9 0.6 copy-done.12
  68.5 0.6 copy-done.13
  69.2 0.6 copy-done.14
  69.8 0.6 copy-done.17
  70.4 15.8 %exchange.3 = (f32[16,8,320]{2,1,0:T(8,128)}, f32[64,320]{1,0:T(8,128)}, f32[64,320]{1,0:T(8,128)}, f32[64,320]{1,0:T(8,128)}, f32[64,320]{1,0:T(8,128)}, /*index=5*/f32[4,8,320]{2,1,0:T(8,128)}) custom-call(f32[8,320]{1,0:T(8,128)} %copy-done.17, f32[64,320]{1,0:T(8,128)} %copy-done.11, f32[64,320]{1,0:T(8,128)} %copy-done.12, f32[64,320]{1,0:T(8,128)} %copy-done.13, ...), custom_call_target="tpu_custom_call" | custom-call | tf_op jit(solution)/shard_map/exchange/pallas_call | solution.py:118
  86.2 0.9 copy-done.18
  87.1 0.9 copy-done.20
  88.0 0.9 copy-done.22
  88.9 0.9 copy-done.24
  89.8 0.9 copy-done.26
  90.7 0.8 copy-done.27
  91.5 16.9 %second.3 = (f32[2048,160]{1,0:T(8,128)}, bf16[2048,128]{1,0:T(8,128)(2,1)S(1)}, bf16[512,128]{1,0:T(8,128)(2,1)S(1)}) custom-call(s32[4]{0:T(128)S(1)} %add_convert_fusion.flags, bf16[4096,320]{1,0:T(8,128)(2,1)} %bitcast.19, bf16[4096,128]{1,0:T(8,128)(2,1)S(1)} %broadcast_in_dim.7.mask_ref, f32[1,320]{1,0:T(1,128)S(1)} %convert_element_type.33.cloud_ref, ...), custom_call_target="tpu_custom_call" | custom-call | flops 6442450944 | bytes 8388608 | tf_op jit(solution)/shard_map/second/pallas_call | solution.py:327
  108.4 0.5 collective-permute-start.2
  109.0 16.9 %second.2 = (f32[2048,160]{1,0:T(8,128)}, bf16[2048,128]{1,0:T(8,128)(2,1)S(1)}, bf16[512,128]{1,0:T(8,128)(2,1)S(1)}) custom-call(s32[4]{0:T(128)S(1)} %add_convert_fusion.flags, bf16[4096,320]{1,0:T(8,128)(2,1)} %bitcast.20, bf16[4096,128]{1,0:T(8,128)(2,1)S(1)} %broadcast_in_dim.7.mask_ref, f32[1,320]{1,0:T(1,128)S(1)} %convert_element_type.33.cloud_ref, ...), custom_call_target="tpu_custom_call" | custom-call | flops 6442450944 | bytes 8388608 | tf_op jit(solution)/shard_map/second/pallas_call | solution.py:327
  125.9 1.5 %collective-permute-start = (bf16[2048,128]{1,0:T(8,128)(2,1)S(1)}, bf16[2048,128]{1,0:T(8,128)(2,1)S(1)}, u32[]{:S(2)}, u32[]{:S(2)}) collective-permute-start(bf16[2048,128]{1,0:T(8,128)(2,1)S(1)} %get-tuple-element.58), channel_id=1, source_target_pairs={{0,16},{16,0},{1,17},{17,1},{2,18},{18,2},{3,19},{19,3},{4,20},{20... | collective-permute-start | bytes 1572872 | tf_op jit(solution)/shard_map/ppermute | solution.py:337
  127.4 0.5 collective-permute-start.3
  127.9 1.5 collective-permute-start.1
  129.4 14.0 %collective-permute-done.3.refs_5_ = bf16[512,128]{1,0:T(8,128)(2,1)S(1)} collective-permute-done((bf16[512,128]{1,0:T(8,128)(2,1)S(1)}, bf16[512,128]{1,0:T(8,128)(2,1)S(1)}, u32[]{:S(2)}, u32[]{:S(2)}) %collective-permute-start.3) | collective-permute-done | bytes 131104 | tf_op jit(solution)/shard_map/ppermute | solution.py:337
  143.4 2.2 %collective-permute-done.1.refs_2_ = bf16[512,128]{1,0:T(8,128)(2,1)S(1)} collective-permute-done((bf16[512,128]{1,0:T(8,128)(2,1)S(1)}, bf16[512,128]{1,0:T(8,128)(2,1)S(1)}, u32[]{:S(2)}, u32[]{:S(2)}) %collective-permute-start.1) | collective-permute-done | bytes 131104 | tf_op jit(solution)/shard_map/ppermute | solution.py:337
  145.7 1.6 %copy-done.1 = f32[2048,160]{1,0:T(8,128)S(1)} copy-done((f32[2048,160]{1,0:T(8,128)S(1)}, f32[2048,160]{1,0:T(8,128)}, u32[]{:S(2)}) %copy-start.1) | copy-done | bytes 1310744
  147.3 3.7 %final.1 = bf16[4096,160]{1,0:T(8,128)(2,1)} custom-call(f32[2048,160]{1,0:T(8,128)S(1)} %copy-done.1, bf16[2048,128]{1,0:T(8,128)(2,1)S(1)} %collective-permute-done.refs_1_, bf16[512,128]{1,0:T(8,128)(2,1)S(1)} %collective-permute-done.1.refs_2_, f32[2048,160]{1,0:T(8,128)} %get-tuple-element.60.refs_3_, ...), custom_call_target="tpu_custom_call" | custom-call | tf_op jit(solution)/shard_map/final/pallas_call | solution.py:338
  (49 shorter events, 0.3 us)
Async XLA Ops:
  0.0 3.8 %copy-start = (bf16[1,320,320]{2,1,0:T(8,128)(2,1)S(1)}, bf16[1,320,320]{2,1,0:T(8,128)(2,1)}, u32[]{:S(2)}) copy-start(bf16[1,320,320]{2,1,0:T(8,128)(2,1)} %param.13) | copy-start | bytes 614404
  4.0 4.9 %copy-start.29 = (bf16[1,2,320]{2,1,0:T(2,128)(2,1)S(1)}, bf16[1,2,320]{2,1,0:T(2,128)(2,1)}, u32[]{:S(2)}) copy-start(bf16[1,2,320]{2,1,0:T(2,128)(2,1)} %param.12) | copy-start | bytes 3844
  14.2 0.6 copy-start.7
  14.8 0.6 copy-start.8
  15.5 0.6 copy-start.9
  16.1 0.6 copy-start.10
  16.7 0.6 copy-start.16
  35.6 0.9 copy-start.2
  36.5 0.9 copy-start.3
  37.4 0.9 copy-start.4
  38.3 0.9 copy-start.5
  39.2 0.9 copy-start.6
  40.1 0.8 copy-start.15
  67.2 0.6 copy-start.11
  67.9 0.7 copy-start.12
  68.5 0.6 copy-start.13
  69.2 0.6 copy-start.14
  69.8 0.6 copy-start.17
  86.2 0.9 copy-start.18
  87.1 0.9 copy-start.20
  88.0 0.9 copy-start.22
  88.9 0.9 copy-start.24
  89.8 0.9 copy-start.26
  90.7 0.8 copy-start.27
  91.5 17.5 %copy-start.19 = (f32[16,8,320]{2,1,0:T(8,128)S(1)}, f32[16,8,320]{2,1,0:T(8,128)}, u32[]{:S(2)}) copy-start(f32[16,8,320]{2,1,0:T(8,128)} %get-tuple-element.51.g_ref) | copy-start | bytes 491524
  91.5 17.5 %copy-start.21 = (f32[64,320]{1,0:T(8,128)S(1)}, f32[64,320]{1,0:T(8,128)}, u32[]{:S(2)}) copy-start(f32[64,320]{1,0:T(8,128)} %get-tuple-element.52.up) | copy-start | bytes 245764
  91.5 17.5 %copy-start.23 = (f32[64,320]{1,0:T(8,128)S(1)}, f32[64,320]{1,0:T(8,128)}, u32[]{:S(2)}) copy-start(f32[64,320]{1,0:T(8,128)} %get-tuple-element.53.down) | copy-start | bytes 245764
  91.5 17.5 %copy-start.25 = (f32[64,320]{1,0:T(8,128)S(1)}, f32[64,320]{1,0:T(8,128)}, u32[]{:S(2)}) copy-start(f32[64,320]{1,0:T(8,128)} %get-tuple-element.54.lft) | copy-start | bytes 245764
  91.5 17.5 %copy-start.28 = (f32[4,8,320]{2,1,0:T(8,128)S(1)}, f32[4,8,320]{2,1,0:T(8,128)}, u32[]{:S(2)}) copy-start(f32[4,8,320]{2,1,0:T(8,128)} %get-tuple-element.56.corner) | copy-start | bytes 122884
  108.4 37.3 %collective-permute-start.2 = (bf16[2048,128]{1,0:T(8,128)(2,1)S(1)}, bf16[2048,128]{1,0:T(8,128)(2,1)S(1)}, u32[]{:S(2)}, u32[]{:S(2)}) collective-permute-start(bf16[2048,128]{1,0:T(8,128)(2,1)S(1)} %get-tuple-element.61), channel_id=1, source_target_pairs={{0,16},{16,0},{1,17},{17,1},{2,18},{18,2},{3,19},{19,3},{4,20},{20... | collective-permute-start | bytes 1572872 | tf_op jit(solution)/shard_map/ppermute | solution.py:337
  125.9 19.8 %collective-permute-start = (bf16[2048,128]{1,0:T(8,128)(2,1)S(1)}, bf16[2048,128]{1,0:T(8,128)(2,1)S(1)}, u32[]{:S(2)}, u32[]{:S(2)}) collective-permute-start(bf16[2048,128]{1,0:T(8,128)(2,1)S(1)} %get-tuple-element.58), channel_id=1, source_target_pairs={{0,16},{16,0},{1,17},{17,1},{2,18},{18,2},{3,19},{19,3},{4,20},{20... | collective-permute-start | bytes 1572872 | tf_op jit(solution)/shard_map/ppermute | solution.py:337
  127.4 16.0 %collective-permute-start.3 = (bf16[512,128]{1,0:T(8,128)(2,1)S(1)}, bf16[512,128]{1,0:T(8,128)(2,1)S(1)}, u32[]{:S(2)}, u32[]{:S(2)}) collective-permute-start(bf16[512,128]{1,0:T(8,128)(2,1)S(1)} %get-tuple-element.62), channel_id=1, source_target_pairs={{0,16},{16,0},{1,17},{17,1},{2,18},{18,2},{3,19},{19,3},{4,20},{20... | collective-permute-start | bytes 393224 | tf_op jit(solution)/shard_map/ppermute | solution.py:337
  127.9 17.8 %collective-permute-start.1 = (bf16[512,128]{1,0:T(8,128)(2,1)S(1)}, bf16[512,128]{1,0:T(8,128)(2,1)S(1)}, u32[]{:S(2)}, u32[]{:S(2)}) collective-permute-start(bf16[512,128]{1,0:T(8,128)(2,1)S(1)} %get-tuple-element.59), channel_id=1, source_target_pairs={{0,16},{16,0},{1,17},{17,1},{2,18},{18,2},{3,19},{19,3},{4,20},{20... | collective-permute-start | bytes 393224 | tf_op jit(solution)/shard_map/ppermute | solution.py:337
  145.7 1.6 %copy-start.1 = (f32[2048,160]{1,0:T(8,128)S(1)}, f32[2048,160]{1,0:T(8,128)}, u32[]{:S(2)}) copy-start(f32[2048,160]{1,0:T(8,128)} %get-tuple-element.57.refs_0_) | copy-start | bytes 3932164

commit v2 on v0

v2 whole, which is shorter than its diff:
```python
import functools
import math

import jax
import jax.numpy as jnp
from jax import lax
from jax.experimental import pallas as pl
from jax.experimental.pallas import tpu as pltpu
from jax.sharding import PartitionSpec as P

GROUPS = 32
EPS = 1e-05
ROWS = 8
MESH = pl.DeviceIdType.MESH
VMEM = pltpu.VMEM


def bf16(*shape):
    return jax.ShapeDtypeStruct(shape, jnp.bfloat16)


def load_inputs(x_ref, mask_ref, cloud_ref, start, count):
    channels = x_ref.shape[1]
    x = x_ref[pl.ds(start, count), :].astype(jnp.float32)
    m = mask_ref[pl.ds(start, count), :].astype(jnp.float32)
    m = jnp.concatenate([m] * pl.cdiv(channels, 128), axis=1)[:, :channels]
    return x + m * cloud_ref[...]


def merge_stats(stat_ref, t, index):
    cells = t.shape[0]
    mean = jnp.sum(t, axis=0, keepdims=True) / cells
    diff = t - mean
    square = jnp.sum(diff * diff, axis=0, keepdims=True)
    k = jnp.asarray(index, jnp.float32)
    delta = mean - stat_ref[0:1, :]
    stat_ref[0:1, :] = stat_ref[0:1, :] + delta / (k + 1.0)
    stat_ref[1:2, :] = stat_ref[1:2, :] + square + delta * delta * (cells * k / (k + 1.0))


def store_columns(t, width, left_ref, right_ref, index):
    t3 = t.reshape(ROWS, width, t.shape[1])
    at = pl.ds(pl.multiple_of(index * ROWS, ROWS), ROWS)
    left_ref[at, :] = t3[:, 0, :]
    right_ref[at, :] = t3[:, width - 1, :]


def split_rows(v):
    high = v.astype(jnp.bfloat16)
    left = v - high.astype(jnp.float32)
    mid = left.astype(jnp.bfloat16)
    low = (left - mid.astype(jnp.float32)).astype(jnp.bfloat16)
    return high, mid, low


def exact_dot(rows, matrix):
    count = rows.shape[0]
    parts = jnp.concatenate([p.astype(jnp.float32) for p in split_rows(rows)], axis=0).astype(jnp.bfloat16)
    y = jnp.dot(parts, matrix, preferred_element_type=jnp.float32)
    return y[0:count] + (y[count:2 * count] + y[2 * count:3 * count])


def group_matrices(channels):
    per = channels // GROUPS

    def member(shape, axis):
        c = lax.broadcasted_iota(jnp.int32, shape, axis)
        g = lax.broadcasted_iota(jnp.int32, shape, 1 - axis)
        return jnp.where((c >= g * per) & (c < g * per + per), 1.0, 0.0).astype(jnp.bfloat16)

    return member((channels, 128), 0), member((128, channels), 1)


def pack_stats(stat_ref, send_ref, cells, matrices):
    to_group, to_channel = matrices
    channels = stat_ref.shape[1]
    per = channels // GROUPS
    mean, square = stat_ref[0:1, :], stat_ref[1:2, :]
    total = exact_dot(jnp.broadcast_to(mean, (8, channels)), to_group)
    off = mean - exact_dot(total / per, to_channel)[0:1, :]
    square = square + cells * off * off
    send_ref[0:8, :] = total / per
    send_ref[8:16, :] = exact_dot(jnp.broadcast_to(square, (8, channels)), to_group)


def group_factors(g_ref, gain, cells, matrices):
    n = g_ref.shape[0]
    per = gain.shape[1] // GROUPS
    means, squares = g_ref[:, 0:8, :], g_ref[:, 8:16, :]
    mean = jnp.sum(means, axis=0) / n
    off = means - mean[None]
    total = jnp.sum(squares, axis=0) + float(cells * per) * jnp.sum(off * off, axis=0)
    inverse = lax.rsqrt(total / (float(cells) * n * per) + EPS)
    return exact_dot(mean, matrices[1])[0:1, :], exact_dot(inverse, matrices[1])[0:1, :] * gain


def kernel(ny, nx, height, width, x_ref, mask_ref, cloud_in, gain_in, embed_ref, mix_ref, w_hbm, out_ref,
           cloud_ref, w_ref, q_ref, mid_ref, keep_ref, out_buf, in_buf, stat_ref, stat_send, gathered,
           row_send, col_send, row_recv, col_recv, corner_recv, w_sem, send, recv, swap_send, swap_recv):
    me_s, me_y, me_x = lax.axis_index("section"), lax.axis_index("gy"), lax.axis_index("gx")
    n = ny * nx
    channels = x_ref.shape[1]
    half = out_ref.shape[1]
    cells = ROWS * width
    chunks = height // ROWS
    other = {"section": 1 - me_s}

    def near(dy, dx):
        return {"gy": lax.rem(me_y + dy + ny, ny), "gx": lax.rem(me_x + dx + nx, nx)}

    barrier = pltpu.get_barrier_semaphore()
    for d in range(1, n):
        pl.semaphore_signal(barrier, inc=1, device_id=near(d // nx, d % nx), device_id_type=MESH)
    pl.semaphore_signal(barrier, inc=1, device_id=other, device_id_type=MESH)
    loads = [pltpu.make_async_copy(w_hbm.at[k], w_ref.at[k], w_sem.at[k]) for k in range(2)]
    for copy in loads:
        copy.start()
    cloud_ref[...] = cloud_in[...].astype(jnp.float32)
    gains = gain_in[0].astype(jnp.float32)
    matrices = group_matrices(channels)
    load = functools.partial(load_inputs, x_ref, mask_ref, cloud_ref)

    def exchange(phase):
        pack_stats(stat_ref, stat_send.at[phase], height * width, matrices)
        rows, cols = row_send.at[phase], col_send.at[phase]
        first, last = pl.ds(0, 8), pl.ds(width - 8, 8)
        corner = corner_recv.at[phase]
        jobs = [
            (cols.at[1], col_recv.at[phase, 0], near(0, 1)),
            (cols.at[0], col_recv.at[phase, 1], near(0, -1)),
            (rows.at[1], row_recv.at[phase, 0], near(1, 0)),
            (rows.at[0], row_recv.at[phase, 1], near(-1, 0)),
            (rows.at[1, last], corner.at[0], near(1, 1)),
            (rows.at[1, first], corner.at[1], near(1, -1)),
            (rows.at[0, last], corner.at[2], near(-1, 1)),
            (rows.at[0, first], corner.at[3], near(-1, -1)),
        ]
        jobs += [(stat_send.at[phase], gathered.at[phase, d], near(d // nx, d % nx)) for d in range(1, n)]
        copies = []
        for k, (src, dst, target) in enumerate(jobs):
            copy = pltpu.make_async_remote_copy(
                src_ref=src, dst_ref=dst, send_sem=send.at[phase, k], recv_sem=recv.at[phase, k],
                device_id=target, device_id_type=MESH,
            )
            copy.start()
            copies.append(copy)
        gathered[phase, 0] = stat_send[phase]
        for copy in copies:
            copy.wait()
        return group_factors(gathered.at[phase], gains[phase:phase + 1], height * width, matrices)

    valid_up, valid_down = me_y > 0, me_y < ny - 1
    valid_left, valid_right = me_x > 0, me_x < nx - 1

    def filler(phase, source, mean, scale):
        def act(t, valid=None):
            z = (t - mean) * scale
            z = z / (1.0 + jnp.exp(-z))
            return z if valid is None else jnp.where(valid, z, 0.0)

        def chunk(i):
            at = pl.ds(pl.multiple_of(i * ROWS, ROWS), ROWS)
            fill_columns(
                q_ref, pl.multiple_of(i * cells + width, width),
                act(source(pl.multiple_of(i * cells, cells), cells)),
                act(col_recv[phase, 0, at, :], valid_left), act(col_recv[phase, 1, at, :], valid_right), ROWS, width,
            )

        def border(k, slot, valid, lcol, rcol):
            fill_columns(
                q_ref, slot * width, act(row_recv[phase, k], valid),
                act(lcol, valid_left & valid), act(rcol, valid_right & valid), 1, width,
            )

        border(0, 0, valid_up, corner_recv[phase, 0, 7:8, :], corner_recv[phase, 1, 0:1, :])
        border(1, height + 1, valid_down, corner_recv[phase, 2, 7:8, :], corner_recv[phase, 3, 0:1, :])
        return chunk

    def run(chunk, step):
        chunk(0)

        def body(i, carry):
            chunk(i + 1)
            step(i)
            return carry

        lax.fori_loop(0, chunks - 1, body, 0)
        step(chunks - 1)

    def observe(phase, t, i):
        merge_stats(stat_ref, t, i)
        store_columns(t, width, col_send.at[phase, 0], col_send.at[phase, 1], i)

    stat_ref[...] = jnp.zeros_like(stat_ref)

    def first_stats(i, carry):
        observe(0, load(pl.multiple_of(i * cells, cells), cells), i)
        return carry

    lax.fori_loop(0, chunks, first_stats, 0)
    row_send[0, 0] = load(0, width)
    row_send[0, 1] = load((height - 1) * width, width)
    pl.semaphore_wait(barrier, n)
    factors = exchange(0)
    stat_ref[...] = jnp.zeros_like(stat_ref)
    loads[0].wait()

    def first_step(i):
        t = conv_chunk(q_ref, w_ref.at[0], i, width) + embed_ref[...]
        mid_ref[pl.ds(pl.multiple_of(i * cells, cells), cells), :] = t
        observe(1, t, i)

    run(filler(0, load, *factors), first_step)
    row_send[1, 0] = mid_ref[0:width, :]
    row_send[1, 1] = mid_ref[(height - 1) * width:, :]
    factors = exchange(1)
    loads[1].wait()
    quarter = cells // 4

    def swap(i):
        return pltpu.make_async_remote_copy(
            src_ref=out_buf.at[i], dst_ref=in_buf.at[i], send_sem=swap_send.at[i], recv_sem=swap_recv.at[i],
            device_id=other, device_id_type=MESH,
        )

    def second_step(i):
        at = pl.ds(pl.multiple_of(i * cells, cells), cells)
        t = load(pl.multiple_of(i * cells, cells), cells)
        skip = (t + conv_chunk(q_ref, w_ref.at[1], i, width)).astype(jnp.bfloat16)
        y = jnp.dot(skip, mix_ref[...], preferred_element_type=jnp.float32)
        out_buf[i, 0:cells, :] = y[:, 256:384].astype(jnp.bfloat16)
        lane = lax.broadcasted_iota(jnp.int32, (quarter, 128), 1)
        rest = y[0:quarter, 384:512]
        for k in range(1, 4):
            rest = jnp.where(lane >= 32 * k, y[k * quarter:(k + 1) * quarter, 384:512], rest)
        out_buf[i, cells:cells + quarter, :] = rest.astype(jnp.bfloat16)
        swap(i).start()
        keep_ref[at, :] = y[:, :half]

    run(filler(1, lambda s, c: mid_ref[pl.ds(s, c), :], *factors), second_step)

    def finish(i, carry):
        swap(i).wait()
        rest = in_buf[i, cells:cells + quarter, :].astype(jnp.float32)
        for k in range(4):
            got = jnp.concatenate(
                [in_buf[i, k * quarter:(k + 1) * quarter, :].astype(jnp.float32), rest[:, 32 * k:32 * k + 32]], axis=1
            )
            at = pl.ds(pl.multiple_of(i * cells + k * quarter, quarter), quarter)
            out_ref[at, :] = (keep_ref[at, :] + got).astype(jnp.bfloat16)
        return carry

    lax.fori_loop(0, chunks, finish, 0)


def fill_columns(q_ref, start, act, lcol, rcol, rows, width):
    channels = act.shape[1]
    v = act.reshape(rows, width, channels)
    col = lax.broadcasted_iota(jnp.int32, v.shape, 1)
    vl = jnp.where(col == 0, lcol.reshape(rows, 1, channels), pltpu.roll(v, 1, 1))
    vr = jnp.where(col == width - 1, rcol.reshape(rows, 1, channels), pltpu.roll(v, width - 1, 1))
    for k, part in enumerate((vl, v, vr)):
        q_ref[pl.ds(start, rows * width), k * channels:(k + 1) * channels] = part.reshape(
            rows * width, channels
        ).astype(jnp.bfloat16)


def conv_chunk(q_ref, w_ref, i, width):
    cells = ROWS * width
    total = None
    for dy in range(3):
        part = jnp.dot(
            q_ref[pl.ds(pl.multiple_of((i * ROWS + dy) * width, width), cells), :],
            w_ref[dy], preferred_element_type=jnp.float32,
        )
        total = part if total is None else total + part
    return total


def per_device(streams, mask, timestep, conv_weight, norm_gain, time_weight, cloud_vec, zero_weight):
    section = lax.axis_index("section")
    ny, nx = lax.axis_size("gy"), lax.axis_size("gx")
    height, width, channels = streams.shape[1:]
    cells = height * width
    half = channels // 2
    freqs = jnp.exp(-math.log(10000.0) * jnp.arange(half, dtype=jnp.float32) / half)
    angles = timestep[0].astype(jnp.float32) * freqs
    sinus = jnp.concatenate([jnp.cos(angles), jnp.sin(angles)]).astype(jnp.bfloat16)
    embed = jax.nn.silu(jnp.dot(sinus[None], time_weight[0], preferred_element_type=jnp.float32))
    x = streams.reshape(cells, channels)
    maskb = jnp.broadcast_to(mask.astype(jnp.bfloat16).reshape(cells, 1), (cells, 128))
    weights = conv_weight.reshape(2, 3, 3 * channels, channels)
    eye = (jnp.arange(channels)[:, None] == (jnp.arange(channels)[None, :] + half) % channels)
    mix = jnp.where(section == 0, zero_weight, eye.astype(jnp.bfloat16))
    tail = mix[:, half + 128:]
    mix = jnp.concatenate(
        [mix[:, :half], jnp.zeros((channels, 256 - half), jnp.bfloat16), mix[:, half:half + 128]] + [tail] * 4, axis=1
    )
    n = ny * nx
    chunks = height // ROWS
    piece = (chunks, ROWS * width * 5 // 4, 128)
    jobs = n - 1 + 8
    dma = pltpu.SemaphoreType.DMA
    vmem = pl.BlockSpec(memory_space=VMEM)
    f4, b2 = jnp.float32, jnp.bfloat16
    out = pl.pallas_call(
        functools.partial(kernel, ny, nx, height, width),
        out_shape=bf16(cells, half),
        in_specs=[vmem] * 6 + [pl.BlockSpec(memory_space=pl.ANY)],
        out_specs=vmem,
        scratch_shapes=[
            VMEM((1, channels), f4), VMEM(weights.shape, b2),
            VMEM(((height + 2) * width, 3 * channels), b2), VMEM((cells, channels), f4),
            VMEM((cells, half), f4), VMEM(piece, b2), VMEM(piece, b2),
            VMEM((8, channels), f4), VMEM((2, 16, 128), f4), VMEM((2, n, 16, 128), f4),
            VMEM((2, 2, width, channels), f4), VMEM((2, 2, height, channels), f4),
            VMEM((2, 2, width, channels), f4), VMEM((2, 2, height, channels), f4), VMEM((2, 4, 8, channels), f4),
            dma((2,)), dma((2, jobs)), dma((2, jobs)), dma((chunks,)), dma((chunks,)),
        ],
        compiler_params=pltpu.CompilerParams(
            collective_id=0, has_side_effects=True, vmem_limit_bytes=56 << 20
        ),
        name="block",
    )(x, maskb, cloud_vec, norm_gain, embed, mix, weights)
    return out.reshape(height, width, half)


def solution(mesh):
    return jax.shard_map(
        per_device,
        mesh=mesh,
        in_specs=(
            P("section", "gy", "gx", None),
            P("gy", "gx"),
            P(),
            P("section", None, None, None, None, None),
            P("section", None, None),
            P("section", None, None),
            P("section", None),
            P(),
        ),
        out_specs=P("gy", "gx", "section"),
        check_vma=False,
    )
```

time: 452 us -> 95.7 us (0.21); the launches traced: 443 us -> 95.5 us
  blocking collectives: 276 us -> 0 us
  Pallas kernels: 0 us -> 85.9 us
  matrix products: 67.1 us -> 0.16 us
  local copies, waits for them, and re-layouts: 48.9 us -> 6.76 us
  other arithmetic: 31.4 us -> 1.94 us
  starting transfers between devices: 16 us -> 0 us
    psum x5 -> x0, blocking collectives: 276 us -> none  [the longest x1 149 us: per_device(): total = lax.psum(term, 'section')]
    pallas_call x0 -> x1, Pallas kernels: none -> 85.9 us  [per_device(): pl.pallas_call(functools.partial(kernel, ny, nx, height, width), out_shap...]
    dot_general x19 -> x0, matrix products: 67 us -> none  [the longest x18 58.2 us: conv_taps(): jnp.dot(window, weight[tap_row, tap_col], preferred_element_type=jnp.floa...]
    slice x5 -> x2, local copies, waits for them, and re-layouts: 17 us -> 0.2 us  [the longest x1 0.11 us: per_device(): mix[:, half:half + 128]]
    ppermute x8 -> x0, starting transfers between devices: 16 us -> none  [the longest x4 10.9 us: padded_2(): before = lax.ppermute(last, axis, up)]
    add x2 -> x0, local copies, waits for them, and re-layouts: 12.7 us -> none  [conv_taps(): summed + jnp.dot(window, weight[tap_row, tap_col], preferred_element_type...]
    convert_element_type x5 -> x1, other arithmetic: 12.1 us -> 0.76 us  [per_device(): mask.astype(jnp.bfloat16).reshape(cells, 1)]
    convert_element_type x3 -> x0, local copies, waits for them, and re-layouts: 10.3 us -> none  [the longest x1 4.59 us: per_device(): skip = (inputs + update).astype(jnp.bfloat16)]
  transfers between devices with their start and end apart: 8 -> 0, of which waited for: 2 -> 0; matrix products, arithmetic and copies ran while one was open for 5% -> 0% of each run, Pallas kernels for 0% -> 0%
where the time goes in v2:
time: 95.7 us; the launch traced here: 95.5 us
  Pallas kernels  85.9 us (90%)
  local copies, waits for them, and re-layouts  6.76 us (7%)
  other arithmetic  1.94 us (2%)
    pallas_call x1, Pallas kernels, per_device(): pl.pallas_call(functools.partial(kernel, ny, nx, height, width), out_shap...  85.9 us
    unnamed x3, local copies, waits for them, and re-layouts  3.28 us

profile of v2, /device:TPU:0, one launch (start us, length us, event | category | flops | bytes accessed | tf_op | source)
XLA Modules:
  0.0 95.5 jit_solution(17522231221523286088)
XLA Ops:
  0.0 0.0 copy-start
  0.7 0.1 sine_convert_fusion
  0.8 0.1 pad_maximum_fusion
  0.8 0.1 copy-done
  1.0 0.2 convolution_reduce_fusion
  1.1 0.6 mul.17.embed_ref
  1.8 0.8 convert_element_type.14
  2.5 0.1 broadcast_in_dim.6
  2.6 1.0 %fusion.1 = bf16[320,320]{1,0:T(8,128)(2,1)S(1)} fusion(bf16[320,320]{1,0:T(8,128)(2,1)} %param.15, s32[320]{0:T(512)S(1)} %add_select_fusion, pred[]{:T(512)S(6)} %eq.18), kind=kLoop, calls=%fused_computation.3 | loop fusion | flops 307200 | bytes 410881 | tf_op jit(solution)/shard_map/jit(_where)/select_n | solution.py:294
  3.6 0.1 slice.15
  3.7 0.1 fusion.6
  3.9 1.0 %concatenate.9.mix_ref = bf16[320,512]{1,0:T(8,128)(2,1)} concatenate(bf16[320,160]{1,0:T(8,128)(2,1)S(1)} %get-tuple-element.6, bf16[320,96]{1,0:T(8,128)(2,1)S(1)} %broadcast_in_dim.15, bf16[320,160]{1,0:T(8,128)(2,1)S(1)} %get-tuple-element.5, bf16[320,32]{1,0:T(8,128)(2,1)S(1)} %slice.15, bf16[320,32]{1,0:T(8,128)(2,1)S(1)} %slice.15, bf16[320,32]{1,0:T(8,128)(2,1)S(1)} %slice.15), dimensions={1} | concatenate | bytes 655360 | tf_op jit(solution)/shard_map/concatenate | solution.py:296
  4.9 1.6 %broadcast_in_dim.14.mask_ref = bf16[4096,128]{1,0:T(8,128)(2,1)} broadcast(bf16[4096]{0:T(1024)(128)(2,1)S(1)} %broadcast_in_dim.6), dimensions={0} | broadcast | bytes 1056768 | tf_op jit(solution)/shard_map/broadcast_in_dim | solution.py:291
  6.4 85.9 %block.1 = bf16[4096,160]{1,0:T(8,128)(2,1)} custom-call(bf16[4096,320]{1,0:T(8,128)(2,1)} %bitcast.10, bf16[4096,128]{1,0:T(8,128)(2,1)} %broadcast_in_dim.14.mask_ref, bf16[1,320]{1,0:T(2,128)(2,1)} %cloud_in.1, bf16[1,2,320]{2,1,0:T(2,128)(2,1)} %gain_in.1, f32[1,320]{1,0:T(1,128)} %mul.17.embed_ref, bf16[320,512]{1,0:T(8,128)(2,1)} %concatenate.9.mix_ref, ...), custom_call_target="tpu_custom_call" | custom-call | tf_op jit(solution)/shard_map/block/pallas_call | solution.py:306
  92.3 3.2 %copy.11 = bf16[64,64,160]{2,1,0:T(8,128)(2,1)} copy(bf16[64,64,160]{2,1,0:T(8,128)(2,1)} %bitcast.8) | data formatting | bytes 2621440
  (4 shorter events, 0.0 us)
Async XLA Ops:
  0.0 1.0 %copy-start = (bf16[1,320,320]{2,1,0:T(8,128)(2,1)S(1)}, bf16[1,320,320]{2,1,0:T(8,128)(2,1)}, u32[]{:S(2)}) copy-start(bf16[1,320,320]{2,1,0:T(8,128)(2,1)} %param.13) | copy-start | bytes 614404

commit v3 on v2

--- a/solution.py
+++ b/solution.py
@@ -79,23 +79,24 @@
     total = exact_dot(jnp.broadcast_to(mean, (8, channels)), to_group)
     off = mean - exact_dot(total / per, to_channel)[0:1, :]
     square = square + cells * off * off
-    send_ref[0:8, :] = total / per
-    send_ref[8:16, :] = exact_dot(jnp.broadcast_to(square, (8, channels)), to_group)
+    squares = exact_dot(jnp.broadcast_to(square, (8, channels)), to_group)
+    row = lax.broadcasted_iota(jnp.int32, (8, 128), 0)
+    send_ref[...] = jnp.where(row < 4, total / per, squares)
 
 
 def group_factors(g_ref, gain, cells, matrices):
     n = g_ref.shape[0]
     per = gain.shape[1] // GROUPS
-    means, squares = g_ref[:, 0:8, :], g_ref[:, 8:16, :]
-    mean = jnp.sum(means, axis=0) / n
-    off = means - mean[None]
-    total = jnp.sum(squares, axis=0) + float(cells * per) * jnp.sum(off * off, axis=0)
-    inverse = lax.rsqrt(total / (float(cells) * n * per) + EPS)
+    values = g_ref[...]
+    mean = jnp.broadcast_to(jnp.sum(values, axis=0)[0:1, :] / n, (8, 128))
+    off = values - mean[None]
+    total = jnp.sum(values, axis=0)[4:5, :] + float(cells * per) * jnp.sum(off * off, axis=0)[0:1, :]
+    inverse = jnp.broadcast_to(lax.rsqrt(total / (float(cells) * n * per) + EPS), (8, 128))
     return exact_dot(mean, matrices[1])[0:1, :], exact_dot(inverse, matrices[1])[0:1, :] * gain
 
 
-def kernel(ny, nx, height, width, x_ref, mask_ref, cloud_in, gain_in, embed_ref, mix_ref, w_hbm, out_ref,
-           cloud_ref, w_ref, q_ref, mid_ref, keep_ref, out_buf, in_buf, stat_ref, stat_send, gathered,
+def kernel(ny, nx, height, width, x_ref, mask_in, cloud_in, gain_in, embed_ref, zero_ref, w_hbm, out_ref,
+           mask_ref, mix_ref, col_sems, cloud_ref, w_ref, q_ref, mid_ref, keep_ref, out_buf, in_buf, stat_ref, stat_send, gathered,
            row_send, col_send, row_recv, col_recv, corner_recv, w_sem, send, recv, swap_send, swap_recv):
     me_s, me_y, me_x = lax.axis_index("section"), lax.axis_index("gy"), lax.axis_index("gx")
     n = ny * nx
@@ -120,32 +121,57 @@
     matrices = group_matrices(channels)
     load = functools.partial(load_inputs, x_ref, mask_ref, cloud_ref)
 
+    first, last = pl.ds(0, 8), pl.ds(width - 8, 8)
+
+    def remote(src, dst, sends, receives, target):
+        return pltpu.make_async_remote_copy(
+            src_ref=src, dst_ref=dst, send_sem=sends, recv_sem=receives,
+            device_id=target, device_id_type=MESH,
+        )
+
+    def column_copies(phase, i):
+        at = pl.ds(pl.multiple_of(i * ROWS, ROWS), ROWS)
+        return [
+            remote(col_send.at[phase, 1, at], col_recv.at[phase, 0, at],
+                   col_sems.at[phase, 0, i], col_sems.at[phase, 1, i], near(0, 1)),
+            remote(col_send.at[phase, 0, at], col_recv.at[phase, 1, at],
+                   col_sems.at[phase, 2, i], col_sems.at[phase, 3, i], near(0, -1)),
+        ]
+
+    def row_copies(phase, side):
+        rows, corner = row_send.at[phase, side], corner_recv.at[phase]
+        dy = 1 if side else -1
+        base = 0 if side else 2
+        jobs = [
+            (rows, row_recv.at[phase, 1 - side], near(dy, 0)),
+            (rows.at[last], corner.at[base], near(dy, 1)),
+            (rows.at[first], corner.at[base + 1], near(dy, -1)),
+        ]
+        return [
+            remote(src, dst, send.at[phase, 3 * side + k], recv.at[phase, 3 * side + k], target)
+            for k, (src, dst, target) in enumerate(jobs)
+        ]
+
+    def stat_copies(phase):
+        return [
+            remote(stat_send.at[phase], gathered.at[phase, d], send.at[phase, 5 + d], recv.at[phase, 5 + d],
+                   near(d // nx, d % nx))
+            for d in range(1, n)
+        ]
+
     def exchange(phase):
         pack_stats(stat_ref, stat_send.at[phase], height * width, matrices)
-        rows, cols = row_send.at[phase], col_send.at[phase]
-        first, last = pl.ds(0, 8), pl.ds(width - 8, 8)
-        corner = corner_recv.at[phase]
-        jobs = [
-            (cols.at[1], col_recv.at[phase, 0], near(0, 1)),
-            (cols.at[0], col_recv.at[phase, 1], near(0, -1)),
-            (rows.at[1], row_recv.at[phase, 0], near(1, 0)),
-            (rows.at[0], row_recv.at[phase, 1], near(-1, 0)),
-            (rows.at[1, last], corner.at[0], near(1, 1)),
-            (rows.at[1, first], corner.at[1], near(1, -1)),
-            (rows.at[0, last], corner.at[2], near(-1, 1)),
-            (rows.at[0, first], corner.at[3], near(-1, -1)),
-        ]
-        jobs += [(stat_send.at[phase], gathered.at[phase, d], near(d // nx, d % nx)) for d in range(1, n)]
-        copies = []
-        for k, (src, dst, target) in enumerate(jobs):
-            copy = pltpu.make_async_remote_copy(
-                src_ref=src, dst_ref=dst, send_sem=send.at[phase, k], recv_sem=recv.at[phase, k],
-                device_id=target, device_id_type=MESH,
-            )
+        for copy in stat_copies(phase):
             copy.start()
-            copies.append(copy)
         gathered[phase, 0] = stat_send[phase]
-        for copy in copies:
+
+        def drain(i, carry):
+            for copy in column_copies(phase, i):
+                copy.wait()
+            return carry
+
+        lax.fori_loop(0, chunks, drain, 0)
+        for copy in row_copies(phase, 0) + row_copies(phase, 1) + stat_copies(phase):
             copy.wait()
         return group_factors(gathered.at[phase], gains[phase:phase + 1], height * width, matrices)
 
@@ -176,31 +202,70 @@
         border(1, height + 1, valid_down, corner_recv[phase, 2, 7:8, :], corner_recv[phase, 3, 0:1, :])
         return chunk
 
-    def run(chunk, step):
+    def run(chunk, step, after=None):
         chunk(0)
+        if after is not None:
+            chunk(1)
+            step(0)
+            after()
+        begin = 0 if after is None else 1
 
         def body(i, carry):
             chunk(i + 1)
             step(i)
             return carry
 
-        lax.fori_loop(0, chunks - 1, body, 0)
+        lax.fori_loop(begin, chunks - 1, body, 0)
         step(chunks - 1)
 
     def observe(phase, t, i):
+        store_columns(t, width, col_send.at[phase, 0], col_send.at[phase, 1], i)
+        for copy in column_copies(phase, i):
+            copy.start()
         merge_stats(stat_ref, t, i)
-        store_columns(t, width, col_send.at[phase, 0], col_send.at[phase, 1], i)
+
+    def send_rows(phase, side, t):
+        row_send[phase, side] = t
+        for copy in row_copies(phase, side):
+            copy.start()
 
     stat_ref[...] = jnp.zeros_like(stat_ref)
+    ones = lax.broadcasted_iota(jnp.int32, (ROWS, ROWS * 128), 1) // 128
+    ones = (ones == lax.broadcasted_iota(jnp.int32, (ROWS, ROWS * 128), 0)).astype(jnp.float32).astype(jnp.bfloat16)
+
+    def spread_mask(i, carry):
+        m = mask_in[pl.ds(pl.multiple_of(i * ROWS, ROWS), ROWS), :].astype(jnp.float32).astype(jnp.bfloat16)
+        wide = lax.dot_general(m, ones, (((0,), (0,)), ((), ())), preferred_element_type=jnp.float32)
+        for r in range(ROWS):
+            at = pl.ds(pl.multiple_of(i * cells + r * width, width), width)
+            mask_ref[at, :] = wide[:, r * 128:(r + 1) * 128].astype(jnp.bfloat16)
+        return carry
+
+    lax.fori_loop(0, chunks, spread_mask, 0)
+    zero = zero_ref[...].astype(jnp.float32)
+    line = lax.broadcasted_iota(jnp.int32, (channels, 1), 0)
+
+    def place(start, stop, count, repeat):
+        lane = lax.broadcasted_iota(jnp.int32, (channels, count), 1)
+        shift = (stop + half) % channels
+        unit = jnp.where(line == lane + shift, 1.0, 0.0)
+        part = jnp.where(me_s == 0, zero[:, stop:stop + count], unit).astype(jnp.float32)
+        part = jnp.concatenate([part] * repeat, axis=1) if repeat > 1 else part
+        mix_ref[:, start:start + count * repeat] = part.astype(jnp.bfloat16)
+
+    mix_ref[:, 128:256] = jnp.zeros((channels, 128), jnp.bfloat16)
+    place(0, 0, half, 1)
+    place(256, half, 128, 1)
+    place(384, half + 128, 32, 4)
+    pl.semaphore_wait(barrier, n)
+    send_rows(0, 0, load(0, width))
+    send_rows(0, 1, load((height - 1) * width, width))
 
     def first_stats(i, carry):
         observe(0, load(pl.multiple_of(i * cells, cells), cells), i)
         return carry
 
     lax.fori_loop(0, chunks, first_stats, 0)
-    row_send[0, 0] = load(0, width)
-    row_send[0, 1] = load((height - 1) * width, width)
-    pl.semaphore_wait(barrier, n)
     factors = exchange(0)
     stat_ref[...] = jnp.zeros_like(stat_ref)
     loads[0].wait()
@@ -210,9 +275,8 @@
         mid_ref[pl.ds(pl.multiple_of(i * cells, cells), cells), :] = t
         observe(1, t, i)
 
-    run(filler(0, load, *factors), first_step)
-    row_send[1, 0] = mid_ref[0:width, :]
-    row_send[1, 1] = mid_ref[(height - 1) * width:, :]
+    run(filler(0, load, *factors), first_step, lambda: send_rows(1, 0, mid_ref[0:width, :]))
+    send_rows(1, 1, mid_ref[(height - 1) * width:, :])
     factors = exchange(1)
     loads[1].wait()
     quarter = cells // 4
@@ -278,7 +342,6 @@
 
 
 def per_device(streams, mask, timestep, conv_weight, norm_gain, time_weight, cloud_vec, zero_weight):
-    section = lax.axis_index("section")
     ny, nx = lax.axis_size("gy"), lax.axis_size("gx")
     height, width, channels = streams.shape[1:]
     cells = height * width
@@ -288,18 +351,11 @@
     sinus = jnp.concatenate([jnp.cos(angles), jnp.sin(angles)]).astype(jnp.bfloat16)
     embed = jax.nn.silu(jnp.dot(sinus[None], time_weight[0], preferred_element_type=jnp.float32))
     x = streams.reshape(cells, channels)
-    maskb = jnp.broadcast_to(mask.astype(jnp.bfloat16).reshape(cells, 1), (cells, 128))
     weights = conv_weight.reshape(2, 3, 3 * channels, channels)
-    eye = (jnp.arange(channels)[:, None] == (jnp.arange(channels)[None, :] + half) % channels)
-    mix = jnp.where(section == 0, zero_weight, eye.astype(jnp.bfloat16))
-    tail = mix[:, half + 128:]
-    mix = jnp.concatenate(
-        [mix[:, :half], jnp.zeros((channels, 256 - half), jnp.bfloat16), mix[:, half:half + 128]] + [tail] * 4, axis=1
-    )
     n = ny * nx
     chunks = height // ROWS
     piece = (chunks, ROWS * width * 5 // 4, 128)
-    jobs = n - 1 + 8
+    jobs = n - 1 + 6
     dma = pltpu.SemaphoreType.DMA
     vmem = pl.BlockSpec(memory_space=VMEM)
     f4, b2 = jnp.float32, jnp.bfloat16
@@ -309,10 +365,11 @@
         in_specs=[vmem] * 6 + [pl.BlockSpec(memory_space=pl.ANY)],
         out_specs=vmem,
         scratch_shapes=[
+            VMEM((cells, 128), b2), VMEM((channels, 512), b2), dma((2, 4, chunks)),
             VMEM((1, channels), f4), VMEM(weights.shape, b2),
             VMEM(((height + 2) * width, 3 * channels), b2), VMEM((cells, channels), f4),
             VMEM((cells, half), f4), VMEM(piece, b2), VMEM(piece, b2),
-            VMEM((8, channels), f4), VMEM((2, 16, 128), f4), VMEM((2, n, 16, 128), f4),
+            VMEM((8, channels), f4), VMEM((2, 8, 128), f4), VMEM((2, n, 8, 128), f4),
             VMEM((2, 2, width, channels), f4), VMEM((2, 2, height, channels), f4),
             VMEM((2, 2, width, channels), f4), VMEM((2, 2, height, channels), f4), VMEM((2, 4, 8, channels), f4),
             dma((2,)), dma((2, jobs)), dma((2, jobs)), dma((chunks,)), dma((chunks,)),
@@ -321,7 +378,7 @@
             collective_id=0, has_side_effects=True, vmem_limit_bytes=56 << 20
         ),
         name="block",
-    )(x, maskb, cloud_vec, norm_gain, embed, mix, weights)
+    )(x, mask, cloud_vec, norm_gain, embed, zero_weight, weights)
     return out.reshape(height, width, half)
 
 

time: 95.7 us -> 84.7 us (0.89)
  Pallas kernels: 85.9 us -> 79.7 us
  local copies, waits for them, and re-layouts: 6.76 us -> 3.87 us
  other arithmetic: 1.94 us -> 0.14 us
    pallas_call x1, Pallas kernels: 85.9 us -> 79.7 us  [per_device(): pl.pallas_call(functools.partial(kernel, ny, nx, height, width), out_shap...]
    broadcast_in_dim x3 -> x0, local copies, waits for them, and re-layouts: 1.68 us -> none  [the longest x2 1.67 us: per_device(): jnp.broadcast_to(mask.astype(jnp.bfloat16).reshape(cells, 1), (cells, 128))]
    select_n x2 -> x0, other arithmetic: 1.05 us -> none  [the longest x1 1.04 us: per_device(): mix = jnp.where(section == 0, zero_weight, eye.astype(jnp.bfloat16))]
    concatenate x1 -> x0, local copies, waits for them, and re-layouts: 0.98 us -> none  [per_device(): jnp.concatenate([mix[:, :half], jnp.zeros((channels, 256 - half), jnp.bfl...]
where the time goes in v3:
time: 84.7 us; the launch traced here: 84.5 us
  Pallas kernels  79.7 us (94%)
  local copies, waits for them, and re-layouts  3.87 us (5%)
    pallas_call x1, Pallas kernels, per_device(): pl.pallas_call(functools.partial(kernel, ny, nx, height, width), out_shap...  79.7 us
    unnamed x3, local copies, waits for them, and re-layouts  3.28 us

profile of v3, /device:TPU:0, one launch (start us, length us, event | category | flops | bytes accessed | tf_op | source)
XLA Modules:
  0.0 84.5 jit_solution(16740533065717812274)
XLA Ops:
  0.0 0.0 copy-start
  0.7 0.1 sine_convert_fusion
  0.8 0.1 pad_maximum_fusion
  0.8 0.1 copy-done
  1.0 0.2 convolution_reduce_fusion
  1.1 0.6 mul.17.embed_ref
  1.7 79.7 %block.1 = bf16[4096,160]{1,0:T(8,128)(2,1)} custom-call(bf16[4096,320]{1,0:T(8,128)(2,1)} %bitcast.10, s32[64,64]{1,0:T(8,128)} %mask_in.1, bf16[1,320]{1,0:T(2,128)(2,1)} %cloud_in.1, bf16[1,2,320]{2,1,0:T(2,128)(2,1)} %gain_in.1, f32[1,320]{1,0:T(1,128)} %mul.17.embed_ref, bf16[320,320]{1,0:T(8,128)(2,1)} %zero_ref.1, bf16[2,3,960,320]{3,2,1,0:T(8,128)(2,1)} %bitcast.9), custom_call_target="tpu_custom_call" | custom-call | tf_op jit(solution)/shard_map/block/pallas_call | solution.py:362
  81.4 3.2 %copy.11 = bf16[64,64,160]{2,1,0:T(8,128)(2,1)} copy(bf16[64,64,160]{2,1,0:T(8,128)(2,1)} %bitcast.8) | data formatting | bytes 2621440
  (2 shorter events, 0.0 us)
Async XLA Ops:
  0.0 1.0 %copy-start = (bf16[1,320,320]{2,1,0:T(8,128)(2,1)S(1)}, bf16[1,320,320]{2,1,0:T(8,128)(2,1)}, u32[]{:S(2)}) copy-start(bf16[1,320,320]{2,1,0:T(8,128)(2,1)} %param.13) | copy-start | bytes 614404

commit v4 on v3

--- a/solution.py
+++ b/solution.py
@@ -202,21 +202,19 @@
         border(1, height + 1, valid_down, corner_recv[phase, 2, 7:8, :], corner_recv[phase, 3, 0:1, :])
         return chunk
 
-    def run(chunk, step, after=None):
+    def run(chunk, compute, emit):
         chunk(0)
-        if after is not None:
-            chunk(1)
-            step(0)
-            after()
-        begin = 0 if after is None else 1
+        chunk(1)
 
         def body(i, carry):
-            chunk(i + 1)
-            step(i)
+            value = compute(i)
+            chunk(i + 2)
+            emit(i, value)
             return carry
 
-        lax.fori_loop(begin, chunks - 1, body, 0)
-        step(chunks - 1)
+        lax.fori_loop(0, chunks - 2, body, 0)
+        for i in (chunks - 2, chunks - 1):
+            emit(i, compute(i))
 
     def observe(phase, t, i):
         store_columns(t, width, col_send.at[phase, 0], col_send.at[phase, 1], i)
@@ -270,12 +268,18 @@
     stat_ref[...] = jnp.zeros_like(stat_ref)
     loads[0].wait()
 
-    def first_step(i):
-        t = conv_chunk(q_ref, w_ref.at[0], i, width) + embed_ref[...]
+    def first_compute(i):
+        return conv_chunk(q_ref, w_ref.at[0], i, width) + embed_ref[...]
+
+    def first_emit(i, t):
         mid_ref[pl.ds(pl.multiple_of(i * cells, cells), cells), :] = t
         observe(1, t, i)
 
-    run(filler(0, load, *factors), first_step, lambda: send_rows(1, 0, mid_ref[0:width, :]))
+        @pl.when(i == 0)
+        def _():
+            send_rows(1, 0, t[0:width, :])
+
+    run(filler(0, load, *factors), first_compute, first_emit)
     send_rows(1, 1, mid_ref[(height - 1) * width:, :])
     factors = exchange(1)
     loads[1].wait()
@@ -287,11 +291,13 @@
             device_id=other, device_id_type=MESH,
         )
 
-    def second_step(i):
-        at = pl.ds(pl.multiple_of(i * cells, cells), cells)
+    def second_compute(i):
         t = load(pl.multiple_of(i * cells, cells), cells)
         skip = (t + conv_chunk(q_ref, w_ref.at[1], i, width)).astype(jnp.bfloat16)
-        y = jnp.dot(skip, mix_ref[...], preferred_element_type=jnp.float32)
+        return jnp.dot(skip, mix_ref[...], preferred_element_type=jnp.float32)
+
+    def second_emit(i, y):
+        at = pl.ds(pl.multiple_of(i * cells, cells), cells)
         out_buf[i, 0:cells, :] = y[:, 256:384].astype(jnp.bfloat16)
         lane = lax.broadcasted_iota(jnp.int32, (quarter, 128), 1)
         rest = y[0:quarter, 384:512]
@@ -301,7 +307,7 @@
         swap(i).start()
         keep_ref[at, :] = y[:, :half]
 
-    run(filler(1, lambda s, c: mid_ref[pl.ds(s, c), :], *factors), second_step)
+    run(filler(1, lambda s, c: mid_ref[pl.ds(s, c), :], *factors), second_compute, second_emit)
 
     def finish(i, carry):
         swap(i).wait()
@@ -375,7 +381,7 @@
             dma((2,)), dma((2, jobs)), dma((2, jobs)), dma((chunks,)), dma((chunks,)),
         ],
         compiler_params=pltpu.CompilerParams(
-            collective_id=0, has_side_effects=True, vmem_limit_bytes=56 << 20
+            collective_id=0, has_side_effects=True, vmem_limit_bytes=44 << 20
         ),
         name="block",
     )(x, mask, cloud_vec, norm_gain, embed, zero_weight, weights)

time: 84.7 us -> 86.1 us (1.017)
  local copies, waits for them, and re-layouts: 3.87 us -> 8.66 us
  Pallas kernels: 79.7 us -> 76.1 us
    unnamed x3 -> x15, local copies, waits for them, and re-layouts: 3.28 us -> 8.65 us
    pallas_call x1, Pallas kernels: 79.7 us -> 76.1 us  [per_device(): pl.pallas_call(functools.partial(kernel, ny, nx, height, width), out_shap...]
where the time goes in v4:
time: 86.1 us; the launch traced here: 85.7 us
  Pallas kernels  76.1 us (88%)
  local copies, waits for them, and re-layouts  8.66 us (10%)
    pallas_call x1, Pallas kernels, per_device(): pl.pallas_call(functools.partial(kernel, ny, nx, height, width), out_shap...  76.1 us
    unnamed x15, local copies, waits for them, and re-layouts  8.65 us

profile of v4, /device:TPU:0, one launch (start us, length us, event | category | flops | bytes accessed | tf_op | source)
XLA Modules:
  0.0 85.7 jit_solution(16962841021040605384)
XLA Ops:
  0.0 0.0 copy-start
  0.7 0.1 sine_convert_fusion
  0.8 0.1 pad_maximum_fusion
  0.8 0.1 copy-done
  1.0 0.2 convolution_reduce_fusion
  1.1 0.0 copy-start.1
  1.2 2.2 %copy-done.1 = bf16[1,2,3,3,320,320]{5,4,3,2,1,0:T(8,128)(2,1)S(1)} copy-done((bf16[1,2,3,3,320,320]{5,4,3,2,1,0:T(8,128)(2,1)S(1)}, bf16[1,2,3,3,320,320]{5,4,3,2,1,0:T(8,128)(2,1)}, u32[]{:S(2)}) %copy-start.1) | copy-done | bytes 3686424
  3.4 0.0 copy-start.2
  3.4 1.9 %copy-done.2 = bf16[1,64,64,320]{3,2,1,0:T(8,128)(2,1)S(1)} copy-done((bf16[1,64,64,320]{3,2,1,0:T(8,128)(2,1)S(1)}, bf16[1,64,64,320]{3,2,1,0:T(8,128)(2,1)}, u32[]{:S(2)}) %copy-start.2) | copy-done | bytes 2621464
  5.3 0.0 copy-start.3
  5.3 0.9 %copy-done.3 = bf16[320,320]{1,0:T(8,128)(2,1)S(1)} copy-done((bf16[320,320]{1,0:T(8,128)(2,1)S(1)}, bf16[320,320]{1,0:T(8,128)(2,1)}, u32[]{:S(2)}) %copy-start.3) | copy-done | bytes 204824
  6.2 0.0 copy-start.4
  6.2 0.8 copy-done.4
  7.0 0.0 copy-start.5
  7.0 0.7 copy-done.5
  7.7 0.0 copy-start.6
  7.7 0.7 copy-done.6
  8.4 76.1 %block.1 = bf16[4096,160]{1,0:T(8,128)(2,1)S(1)} custom-call(bf16[4096,320]{1,0:T(8,128)(2,1)S(1)} %bitcast.10, s32[64,64]{1,0:T(8,128)S(1)} %copy-done.4, bf16[1,320]{1,0:T(2,128)(2,1)S(1)} %copy-done.5, bf16[1,2,320]{2,1,0:T(2,128)(2,1)S(1)} %copy-done.6, f32[1,320]{1,0:T(1,128)S(1)} %mul.17.embed_ref, bf16[320,320]{1,0:T(8,128)(2,1)S(1)} %copy-done.3, ...), custom_call_target="tpu_custom_call" | custom-call | tf_op jit(solution)/shard_map/block/pallas_call | solution.py:368
  84.4 1.3 %copy.11 = bf16[64,64,160]{2,1,0:T(8,128)(2,1)} copy(bf16[64,64,160]{2,1,0:T(8,128)(2,1)S(1)} %bitcast.8) | data formatting | bytes 2621440
  (3 shorter events, 0.0 us)
Async XLA Ops:
  0.0 1.0 %copy-start = (bf16[1,320,320]{2,1,0:T(8,128)(2,1)S(1)}, bf16[1,320,320]{2,1,0:T(8,128)(2,1)}, u32[]{:S(2)}) copy-start(bf16[1,320,320]{2,1,0:T(8,128)(2,1)} %param.13) | copy-start | bytes 614404
  1.1 2.3 %copy-start.1 = (bf16[1,2,3,3,320,320]{5,4,3,2,1,0:T(8,128)(2,1)S(1)}, bf16[1,2,3,3,320,320]{5,4,3,2,1,0:T(8,128)(2,1)}, u32[]{:S(2)}) copy-start(bf16[1,2,3,3,320,320]{5,4,3,2,1,0:T(8,128)(2,1)} %param.11) | copy-start | bytes 11059204
  3.4 1.9 %copy-start.2 = (bf16[1,64,64,320]{3,2,1,0:T(8,128)(2,1)S(1)}, bf16[1,64,64,320]{3,2,1,0:T(8,128)(2,1)}, u32[]{:S(2)}) copy-start(bf16[1,64,64,320]{3,2,1,0:T(8,128)(2,1)} %param.8) | copy-start | bytes 7864324
  5.3 0.9 %copy-start.3 = (bf16[320,320]{1,0:T(8,128)(2,1)S(1)}, bf16[320,320]{1,0:T(8,128)(2,1)}, u32[]{:S(2)}) copy-start(bf16[320,320]{1,0:T(8,128)(2,1)} %zero_ref.1) | copy-start | bytes 614404
  6.2 0.8 copy-start.4
  7.0 0.7 copy-start.5
  7.7 0.7 copy-start.6

commit v5 on v4

--- a/solution.py
+++ b/solution.py
@@ -95,8 +95,8 @@
     return exact_dot(mean, matrices[1])[0:1, :], exact_dot(inverse, matrices[1])[0:1, :] * gain
 
 
-def kernel(ny, nx, height, width, x_ref, mask_in, cloud_in, gain_in, embed_ref, zero_ref, w_hbm, out_ref,
-           mask_ref, mix_ref, col_sems, cloud_ref, w_ref, q_ref, mid_ref, keep_ref, out_buf, in_buf, stat_ref, stat_send, gathered,
+def kernel(ny, nx, height, width, x_hbm, mask_hbm, cloud_in, gain_in, embed_ref, zero_hbm, w_hbm, out_ref,
+           x_ref, mask_in, zero_ref, mask_ref, mix_ref, col_sems, cloud_ref, w_ref, q_ref, mid_ref, keep_ref, out_buf, in_buf, stat_ref, stat_send, gathered,
            row_send, col_send, row_recv, col_recv, corner_recv, w_sem, send, recv, swap_send, swap_recv):
     me_s, me_y, me_x = lax.axis_index("section"), lax.axis_index("gy"), lax.axis_index("gx")
     n = ny * nx
@@ -113,7 +113,13 @@
     for d in range(1, n):
         pl.semaphore_signal(barrier, inc=1, device_id=near(d // nx, d % nx), device_id_type=MESH)
     pl.semaphore_signal(barrier, inc=1, device_id=other, device_id_type=MESH)
-    loads = [pltpu.make_async_copy(w_hbm.at[k], w_ref.at[k], w_sem.at[k]) for k in range(2)]
+    loads = [
+        pltpu.make_async_copy(src, dst, w_sem.at[k])
+        for k, (src, dst) in enumerate((
+            (mask_hbm, mask_in), (zero_hbm, zero_ref), (x_hbm, x_ref),
+            (w_hbm.at[0], w_ref.at[0]), (w_hbm.at[1], w_ref.at[1]),
+        ))
+    ]
     for copy in loads:
         copy.start()
     cloud_ref[...] = cloud_in[...].astype(jnp.float32)
@@ -228,6 +234,7 @@
             copy.start()
 
     stat_ref[...] = jnp.zeros_like(stat_ref)
+    loads[0].wait()
     ones = lax.broadcasted_iota(jnp.int32, (ROWS, ROWS * 128), 1) // 128
     ones = (ones == lax.broadcasted_iota(jnp.int32, (ROWS, ROWS * 128), 0)).astype(jnp.float32).astype(jnp.bfloat16)
 
@@ -240,6 +247,7 @@
         return carry
 
     lax.fori_loop(0, chunks, spread_mask, 0)
+    loads[1].wait()
     zero = zero_ref[...].astype(jnp.float32)
     line = lax.broadcasted_iota(jnp.int32, (channels, 1), 0)
 
@@ -255,6 +263,7 @@
     place(0, 0, half, 1)
     place(256, half, 128, 1)
     place(384, half + 128, 32, 4)
+    loads[2].wait()
     pl.semaphore_wait(barrier, n)
     send_rows(0, 0, load(0, width))
     send_rows(0, 1, load((height - 1) * width, width))
@@ -266,7 +275,7 @@
     lax.fori_loop(0, chunks, first_stats, 0)
     factors = exchange(0)
     stat_ref[...] = jnp.zeros_like(stat_ref)
-    loads[0].wait()
+    loads[3].wait()
 
     def first_compute(i):
         return conv_chunk(q_ref, w_ref.at[0], i, width) + embed_ref[...]
@@ -282,7 +291,7 @@
     run(filler(0, load, *factors), first_compute, first_emit)
     send_rows(1, 1, mid_ref[(height - 1) * width:, :])
     factors = exchange(1)
-    loads[1].wait()
+    loads[4].wait()
     quarter = cells // 4
 
     def swap(i):
@@ -364,13 +373,15 @@
     jobs = n - 1 + 6
     dma = pltpu.SemaphoreType.DMA
     vmem = pl.BlockSpec(memory_space=VMEM)
+    hbm = pl.BlockSpec(memory_space=pltpu.HBM)
     f4, b2 = jnp.float32, jnp.bfloat16
     out = pl.pallas_call(
         functools.partial(kernel, ny, nx, height, width),
         out_shape=bf16(cells, half),
-        in_specs=[vmem] * 6 + [pl.BlockSpec(memory_space=pl.ANY)],
+        in_specs=[hbm, hbm, vmem, vmem, vmem, hbm, hbm],
         out_specs=vmem,
         scratch_shapes=[
+            VMEM((cells, channels), b2), VMEM(mask.shape, jnp.int32), VMEM(zero_weight.shape, b2),
             VMEM((cells, 128), b2), VMEM((channels, 512), b2), dma((2, 4, chunks)),
             VMEM((1, channels), f4), VMEM(weights.shape, b2),
             VMEM(((height + 2) * width, 3 * channels), b2), VMEM((cells, channels), f4),
@@ -378,7 +389,7 @@
             VMEM((8, channels), f4), VMEM((2, 8, 128), f4), VMEM((2, n, 8, 128), f4),
             VMEM((2, 2, width, channels), f4), VMEM((2, 2, height, channels), f4),
             VMEM((2, 2, width, channels), f4), VMEM((2, 2, height, channels), f4), VMEM((2, 4, 8, channels), f4),
-            dma((2,)), dma((2, jobs)), dma((2, jobs)), dma((chunks,)), dma((chunks,)),
+            dma((5,)), dma((2, jobs)), dma((2, jobs)), dma((chunks,)), dma((chunks,)),
         ],
         compiler_params=pltpu.CompilerParams(
             collective_id=0, has_side_effects=True, vmem_limit_bytes=44 << 20

time: 86.1 us -> 86.1 us (level)
  no operation moved by 1% of the time
where the time goes in v5:
time: 86.1 us; the launch traced here: 85.8 us
  Pallas kernels  76.1 us (88%)
  local copies, waits for them, and re-layouts  8.66 us (10%)
    pallas_call x1, Pallas kernels, per_device(): pl.pallas_call(functools.partial(kernel, ny, nx, height, width), out_shap...  76.1 us
    unnamed x15, local copies, waits for them, and re-layouts  8.65 us

profile of v5, /device:TPU:0, one launch (start us, length us, event | category | flops | bytes accessed | tf_op | source)
XLA Modules:
  0.0 85.8 jit_solution(911327043547446655)
XLA Ops:
  0.0 0.0 copy-start
  0.7 0.1 sine_convert_fusion
  0.8 0.1 pad_maximum_fusion
  0.8 0.1 copy-done
  1.0 0.2 convolution_reduce_fusion
  1.1 0.0 copy-start.1
  1.2 2.2 %copy-done.1 = bf16[1,2,3,3,320,320]{5,4,3,2,1,0:T(8,128)(2,1)S(1)} copy-done((bf16[1,2,3,3,320,320]{5,4,3,2,1,0:T(8,128)(2,1)S(1)}, bf16[1,2,3,3,320,320]{5,4,3,2,1,0:T(8,128)(2,1)}, u32[]{:S(2)}) %copy-start.1) | copy-done | bytes 3686424
  3.4 0.0 copy-start.2
  3.4 1.9 %copy-done.2 = bf16[1,64,64,320]{3,2,1,0:T(8,128)(2,1)S(1)} copy-done((bf16[1,64,64,320]{3,2,1,0:T(8,128)(2,1)S(1)}, bf16[1,64,64,320]{3,2,1,0:T(8,128)(2,1)}, u32[]{:S(2)}) %copy-start.2) | copy-done | bytes 2621464
  5.3 0.0 copy-start.3
  5.3 0.9 %copy-done.3 = bf16[320,320]{1,0:T(8,128)(2,1)S(1)} copy-done((bf16[320,320]{1,0:T(8,128)(2,1)S(1)}, bf16[320,320]{1,0:T(8,128)(2,1)}, u32[]{:S(2)}) %copy-start.3) | copy-done | bytes 204824
  6.2 0.0 copy-start.4
  6.2 0.8 copy-done.4
  7.0 0.0 copy-start.5
  7.0 0.7 copy-done.5
  7.7 0.0 copy-start.6
  7.7 0.7 copy-done.6
  8.4 76.1 %block.1 = bf16[4096,160]{1,0:T(8,128)(2,1)S(1)} custom-call(bf16[4096,320]{1,0:T(8,128)(2,1)S(1)} %bitcast.10, s32[64,64]{1,0:T(8,128)S(1)} %copy-done.4, bf16[1,320]{1,0:T(2,128)(2,1)S(1)} %copy-done.5, bf16[1,2,320]{2,1,0:T(2,128)(2,1)S(1)} %copy-done.6, f32[1,320]{1,0:T(1,128)S(1)} %mul.17.embed_ref, bf16[320,320]{1,0:T(8,128)(2,1)S(1)} %copy-done.3, ...), custom_call_target="tpu_custom_call" | custom-call | tf_op jit(solution)/shard_map/block/pallas_call | solution.py:378
  84.5 1.3 %copy.11 = bf16[64,64,160]{2,1,0:T(8,128)(2,1)} copy(bf16[64,64,160]{2,1,0:T(8,128)(2,1)S(1)} %bitcast.8) | data formatting | bytes 2621440
  (3 shorter events, 0.0 us)
Async XLA Ops:
  0.0 1.0 %copy-start = (bf16[1,320,320]{2,1,0:T(8,128)(2,1)S(1)}, bf16[1,320,320]{2,1,0:T(8,128)(2,1)}, u32[]{:S(2)}) copy-start(bf16[1,320,320]{2,1,0:T(8,128)(2,1)} %param.13) | copy-start | bytes 614404
  1.1 2.3 %copy-start.1 = (bf16[1,2,3,3,320,320]{5,4,3,2,1,0:T(8,128)(2,1)S(1)}, bf16[1,2,3,3,320,320]{5,4,3,2,1,0:T(8,128)(2,1)}, u32[]{:S(2)}) copy-start(bf16[1,2,3,3,320,320]{5,4,3,2,1,0:T(8,128)(2,1)} %param.11) | copy-start | bytes 11059204
  3.4 1.9 %copy-start.2 = (bf16[1,64,64,320]{3,2,1,0:T(8,128)(2,1)S(1)}, bf16[1,64,64,320]{3,2,1,0:T(8,128)(2,1)}, u32[]{:S(2)}) copy-start(bf16[1,64,64,320]{3,2,1,0:T(8,128)(2,1)} %param.8) | copy-start | bytes 7864324
  5.3 0.9 %copy-start.3 = (bf16[320,320]{1,0:T(8,128)(2,1)S(1)}, bf16[320,320]{1,0:T(8,128)(2,1)}, u32[]{:S(2)}) copy-start(bf16[320,320]{1,0:T(8,128)(2,1)} %zero_hbm.1) | copy-start | bytes 614404
  6.2 0.8 copy-start.4
  7.0 0.7 copy-start.5
  7.7 0.7 copy-start.6
